TPU v7x, 32 devices: a whole 2x2x4 slice. The times are simulated.
32 devices in a mesh: clip: 4 (over z), wide: 4 (over y, core), narrow: 2 (over x).
Axes of the slice: x: 2, y: 2, z: 4, core: 2. Of those that a mesh axis runs over, the one named last changes fastest.
Arguments:
- tokens: bfloat16 [4, 1024, 1536], P('clip', ('wide', 'narrow')), may hold values from -6 to 6
- positions: int32 [4, 1024], P('clip', ('wide', 'narrow')), may hold values from 0 to 1023, each once within a row
- captions: bfloat16 [4, 256, 4096], P('clip', 'narrow'), may hold values from -6 to 6
- caption_lengths: int32 [4], replicated, may hold values from 1 to 256, 640 in all
- conditioning: bfloat16 [4, 1024], P(None, ('clip', 'wide', 'narrow')), may hold values from -6 to 6
- modulation_weight: bfloat16 [1024, 9216], P(('clip', 'wide', 'narrow')), may hold values from -0.1875 to 0.1875
- modulation_bias: float32 [9216], replicated, may hold values from -3 to 3
- attention_gain: float32 [1536], replicated, may hold values from 0.5 to 1.5
- query_weight: bfloat16 [1536, 1536], P(('clip', 'wide', 'narrow')), may hold values from -0.15625 to 0.15625
- key_weight: bfloat16 [1536, 1536], P(('clip', 'wide', 'narrow')), may hold values from -0.15625 to 0.15625
- value_weight: bfloat16 [1536, 1536], P(('clip', 'wide', 'narrow')), may hold values from -0.15625 to 0.15625
- query_gain: float32 [64], replicated, may hold values from 0.5 to 1.5
- key_gain: float32 [64], replicated, may hold values from 0.5 to 1.5
- text_weight: bfloat16 [4096, 1536], P(('clip', 'wide', 'narrow')), may hold values from -0.09375 to 0.09375
- textkey_weight: bfloat16 [1536, 1536], P(('clip', 'wide', 'narrow')), may hold values from -0.15625 to 0.15625
- textvalue_weight: bfloat16 [1536, 1536], P(('clip', 'wide', 'narrow')), may hold values from -0.15625 to 0.15625
- textkey_gain: float32 [64], replicated, may hold values from 0.5 to 1.5
- cross_gate: float32 [24], replicated, may hold values from -0.25 to 0.25
- output_weight: bfloat16 [1536, 1536], P(('clip', 'wide', 'narrow')), may hold values from -4 to 4
- feedforward_gain: float32 [1536], replicated, may hold values from 0.5 to 1.5
- gate_weight: bfloat16 [1536, 4096], P(('clip', 'wide', 'narrow')), may hold values from -0.15625 to 0.15625
- up_weight: bfloat16 [1536, 4096], P(('clip', 'wide', 'narrow')), may hold values from -0.15625 to 0.15625
- down_weight: bfloat16 [4096, 1536], P(('clip', 'wide', 'narrow')), may hold values from -0.09375 to 0.09375
- cotangent: bfloat16 [4, 1024, 1536], P('clip', ('wide', 'narrow')), may hold values from -6 to 6
Outputs:
- block_output: float32 [4, 1024, 1536], P('clip', ('wide', 'narrow'))
- tokens_grad: float32 [4, 1024, 1536], P('clip', ('wide', 'narrow'))
- captions_grad: float32 [4, 256, 4096], P('clip', 'narrow')
- conditioning_grad: float32 [4, 1024], P(None, ('clip', 'wide', 'narrow'))
- modweight_grad: float32 [1024, 9216], P(('clip', 'wide', 'narrow'))
- modbias_grad: float32 [9216], replicated
- attngain_grad: float32 [1536], replicated
- queryweight_grad: float32 [1536, 1536], P(('clip', 'wide', 'narrow'))
- keyweight_grad: float32 [1536, 1536], P(('clip', 'wide', 'narrow'))
- valueweight_grad: float32 [1536, 1536], P(('clip', 'wide', 'narrow'))
- querygain_grad: float32 [64], replicated
- keygain_grad: float32 [64], replicated
- textweight_grad: float32 [4096, 1536], P(('clip', 'wide', 'narrow'))
- textkey_grad: float32 [1536, 1536], P(('clip', 'wide', 'narrow'))
- textvalue_grad: float32 [1536, 1536], P(('clip', 'wide', 'narrow'))
- textgain_grad: float32 [64], replicated
- crossgate_grad: float32 [24], replicated
- outweight_grad: float32 [1536, 1536], P(('clip', 'wide', 'narrow'))
- feedgain_grad: float32 [1536], replicated
- gateweight_grad: float32 [1536, 4096], P(('clip', 'wide', 'narrow'))
- upweight_grad: float32 [1536, 4096], P(('clip', 'wide', 'narrow'))
- downweight_grad: float32 [4096, 1536], P(('clip', 'wide', 'narrow'))
Inputs may be any that keep to these rules, and one draw needn't show every extreme that they name: Each clip's positions are a permutation of 0 to 1023. `caption_lengths`: some clip has all 256 caption slots live.
All inputs are finite; a program needn't handle non-finite values.
Results may differ from a plain program's by a relative error of at most 0.025.
Values may be sent and summed in bfloat16 or wider, within the bound.
No kernel may reach another device: no remote copies, remote signals or barrier semaphores. Data moves between devices by JAX's collectives and lax.ppermute only.
A program may use at most 384 MiB of HBM per device.

v0:
```python
import math

import jax
import jax.numpy as jnp
from jax import lax
from jax.sharding import PartitionSpec as P

EPSILON = 1e-06
ROPE_BASE = 10000.0
C, W, N = "clip", "wide", "narrow"
ALL = (C, W, N)
PLANE = (W, N)
BF16, F32 = jnp.bfloat16, jnp.float32
HIGHEST = lax.Precision.HIGHEST


def dot(left, right, left_dim=1, right_dim=0):
    return lax.dot_general(
        left, right, (((left_dim,), (right_dim,)), ((), ())), preferred_element_type=F32
    )


def inverse_rms(values):
    return lax.rsqrt(jnp.mean(values * values, axis=-1, keepdims=True) + EPSILON)


def norm_backward(normed, inv_scale, gain, upstream):
    gain_grad = jnp.sum((upstream * normed).reshape(-1, normed.shape[-1]), axis=0)
    scaled = upstream * gain
    values_grad = inv_scale * (scaled - normed * jnp.mean(scaled * normed, axis=-1, keepdims=True))
    return (gain_grad, values_grad)


def rope_tables(positions, head_size):
    half_size = head_size // 2
    frequency = jnp.exp(-math.log(ROPE_BASE) * 2.0 * jnp.arange(half_size, dtype=F32) / head_size)
    angles = positions.astype(F32)[:, None] * frequency[None, :]
    return (jnp.cos(angles)[:, None, :], jnp.sin(angles)[:, None, :])


def rotate(values, cosine_table, sine_table):
    half_size = values.shape[-1] // 2
    first_half = values[..., :half_size]
    second_half = values[..., half_size:]
    return jnp.concatenate(
        [
            first_half * cosine_table - second_half * sine_table,
            first_half * sine_table + second_half * cosine_table,
        ],
        axis=-1,
    )


def axes_size(axes):
    return math.prod(lax.axis_size(axis) for axis in axes)


def swap(x, axes, mask):
    return lax.ppermute(x, axes, [(i, i ^ mask) for i in range(axes_size(axes))])


def pick(x, index, axis=0):
    return lax.dynamic_index_in_dim(x, index, axis, keepdims=False)


def spread(x, axes, masks):
    fast, first, second = masks
    me = lax.axis_index(axes)
    rows = x.shape[0]
    half = rows // 2
    one = swap(x, axes, first)
    two = swap(x, axes, second)
    if half:
        far = jnp.concatenate(
            [swap(two[:half], axes, first), swap(one[half:], axes, second)], axis=0
        )
    else:
        far = swap(two, axes, first)
    held = {0: x, first: one, second: two, first ^ second: far}
    for mask in (0, first, second, first ^ second):
        held[mask ^ fast] = swap(held[mask], axes, fast)
    out = jnp.zeros((len(held),) + x.shape, x.dtype)
    for mask, piece in held.items():
        out = lax.dynamic_update_index_in_dim(out, piece, me ^ mask, 0)
    return out


def collect(parts, axes, masks):
    fast, first, second = masks
    me = lax.axis_index(axes)
    rows = parts.shape[1]
    half = rows // 2

    def low(x):
        return x.astype(BF16)

    def part(mask):
        return pick(parts, me ^ mask)

    total = {}
    for mask in (first ^ second, first, second, 0):
        got = swap(low(part(mask ^ fast)), axes, fast)
        total[mask] = part(mask).astype(F32) + got.astype(F32)
    far, one, two, own = total[first ^ second], total[first], total[second], total[0]
    to_two = swap(low(far[:half]), axes, first)
    to_one = swap(low(far[half:]), axes, second)
    one_low = swap(low(one[:half]), axes, first)
    two_high = swap(low(two[half:]), axes, second)
    two_low = swap(low(two[:half] + to_two.astype(F32)), axes, second)
    one_high = swap(low(one[half:] + to_one.astype(F32)), axes, first)
    low_rows = own[:half] + one_low.astype(F32) + two_low.astype(F32)
    high_rows = own[half:] + one_high.astype(F32) + two_high.astype(F32)
    return jnp.concatenate([low_rows, high_rows], axis=0)


def small_sum(x, axes):
    count = axes_size(axes)
    if count > 8 or count & (count - 1):
        return lax.psum(x, axes)
    total = x
    for mask in range(1, count):
        total = total + swap(x, axes, mask)
    return total


def clip_rows(x, axes):
    count = axes_size(axes)
    if count > 8 or count & (count - 1):
        return lax.psum_scatter(x, axes, scatter_dimension=0, tiled=False)
    me = lax.axis_index(axes)
    total = pick(x, me).astype(F32)
    for mask in range(1, count):
        total = total + swap(pick(x, me ^ mask), axes, mask).astype(F32)
    return total


def clip_spread(x, axes):
    count = axes_size(axes)
    if count > 8 or count & (count - 1):
        return lax.all_gather(x, axes, axis=0, tiled=False)
    me = lax.axis_index(axes)
    out = jnp.zeros((count,) + x.shape, x.dtype)
    for mask in range(count):
        piece = swap(x, axes, mask) if mask else x
        out = lax.dynamic_update_index_in_dim(out, piece, me ^ mask, 0)
    return out


def turn(x, axes):
    return lax.all_to_all(x, axes, split_axis=0, concat_axis=0, tiled=False)


def on_device(
    tokens,
    positions,
    captions,
    caption_lengths,
    conditioning,
    modulation_weight,
    modulation_bias,
    attention_gain,
    query_weight,
    key_weight,
    value_weight,
    query_gain,
    key_gain,
    text_weight,
    textkey_weight,
    textvalue_weight,
    textkey_gain,
    cross_gate,
    output_weight,
    feedforward_gain,
    gate_weight,
    up_weight,
    down_weight,
    cotangent,
):
    wide_count, narrow_count = lax.axis_size(W), lax.axis_size(N)
    clip_count = lax.axis_size(C)
    clip_index, wide_index = lax.axis_index(C), lax.axis_index(W)
    own_rows, model_width = tokens.shape[1], tokens.shape[2]
    head_size = query_gain.shape[0]
    head_count = model_width // head_size
    score_scale = head_size ** (-0.5)
    score_shift = 3.0 * math.sqrt(head_size)
    split_tokens = head_count % (wide_count * narrow_count) != 0
    tp, dp = ((N,), (C, W)) if split_tokens else (PLANE, (C,))
    tp_count, dp_count = axes_size(tp), axes_size(dp)
    tp_index = lax.axis_index(tp)
    masks = (2, 1, 4)
    group_rows = own_rows * tp_count
    local_heads = head_count // tp_count
    head_width = local_heads * head_size
    weight_rows = query_weight.shape[0]
    hidden_rows, hidden_width = down_weight.shape[0], gate_weight.shape[1]
    local_hidden = hidden_width // tp_count

    cond_float = conditioning.astype(F32)
    cond_act = jax.nn.silu(cond_float)
    weight_float = modulation_weight.astype(F32)
    partial_mod = jnp.dot(cond_act, weight_float, precision=HIGHEST, preferred_element_type=F32)
    own_mod = small_sum(clip_rows(partial_mod, (C,)), PLANE) + modulation_bias
    shift_attn, scale_attn, gate_attn, shift_feed, scale_feed, gate_feed = jnp.split(own_mod, 6)

    def head_columns(weight):
        return weight.reshape(weight_rows, tp_count, head_width).transpose(1, 0, 2)

    def hidden_columns(weight):
        split = weight.reshape(weight_rows, dp_count, tp_count, hidden_rows)
        return split.transpose(2, 0, 1, 3).reshape(tp_count, weight_rows, local_hidden)

    def gather_rows(rows):
        return lax.all_gather(rows, dp, axis=0, tiled=True)

    qkv_parts = turn(
        jnp.concatenate([head_columns(w) for w in (query_weight, key_weight, value_weight)], axis=2), tp
    )
    qkv_slice = gather_rows(qkv_parts.reshape(tp_count * weight_rows, 3 * head_width))
    text_parts = turn(
        jnp.concatenate([head_columns(w) for w in (textkey_weight, textvalue_weight)], axis=2), tp
    ).reshape(tp_count * weight_rows, 2 * head_width)
    pieces = model_width // (2 * head_width)
    mixed_rows = jnp.concatenate(
        [text_parts, output_weight.reshape(weight_rows * pieces, 2 * head_width)], axis=0
    )
    mixed_all = gather_rows(mixed_rows).reshape(dp_count, mixed_rows.shape[0], 2 * head_width)
    text_slice = mixed_all[:, : tp_count * weight_rows].reshape(model_width, 2 * head_width)
    output_rows = mixed_all[:, tp_count * weight_rows :].reshape(dp_count * weight_rows, model_width)
    output_all = spread(output_rows, tp, masks).reshape(tp_count, dp_count, weight_rows, model_width)
    output_full = output_all.transpose(1, 0, 2, 3).reshape(model_width, model_width)
    hidden_parts = turn(
        jnp.concatenate([hidden_columns(gate_weight), hidden_columns(up_weight)], axis=2), tp
    )
    hidden_slice = gather_rows(hidden_parts.reshape(tp_count * weight_rows, 2 * local_hidden))
    down_slice = gather_rows(down_weight)

    token_all = spread(tokens[0], tp, masks).reshape(group_rows, model_width)
    cotangent_all = spread(cotangent[0], tp, masks).reshape(group_rows, model_width)
    position_all = spread(positions, tp, masks).reshape(group_rows)

    token_float = tokens[0].astype(F32)
    inv_attn = inverse_rms(token_float)
    hat_attn = token_float * inv_attn
    normed_attn = hat_attn * attention_gain
    group_float = token_all.astype(F32)
    group_normed = group_float * inverse_rms(group_float) * attention_gain
    mod_in = (group_normed * (1.0 + scale_attn) + shift_attn).astype(BF16)

    caption_rows, text_width = captions.shape[1], captions.shape[2]
    text_rows = text_weight.shape[0]
    own_columns = pick(
        captions[0].reshape(caption_rows, clip_count, wide_count, narrow_count, text_rows), wide_index, 2
    )
    caption_parts = own_columns.transpose(1, 2, 0, 3).reshape(-1, caption_rows, text_rows)
    caption_columns = turn(caption_parts, (C, N)).reshape(-1, text_rows)
    slot_count = caption_rows * narrow_count
    slot_part = slot_count // tp_count
    text_partial = dot(caption_columns, text_weight).reshape(clip_count, tp_count, slot_part, model_width)
    text_group = collect(
        text_partial.transpose(1, 0, 2, 3).reshape(tp_count, clip_count * slot_part, model_width), tp, masks
    )
    if split_tokens:
        text_group = lax.psum(text_group, W)
    text_own = clip_rows(text_group.astype(BF16).reshape(clip_count, slot_part, model_width), (C,))
    text_proj = spread(text_own.astype(BF16), tp, masks).reshape(slot_count, model_width)

    heads_shape = (group_rows, local_heads, head_size)
    cosine_table, sine_table = rope_tables(position_all, head_size)
    qkv_raw = dot(mod_in, qkv_slice)
    query_raw = qkv_raw[:, :head_width].reshape(heads_shape)
    key_raw = qkv_raw[:, head_width : 2 * head_width].reshape(heads_shape)
    value_heads = qkv_raw[:, 2 * head_width :].astype(BF16).reshape(heads_shape)
    inv_query = inverse_rms(query_raw)
    hat_query = query_raw * inv_query
    query_rot = rotate(hat_query * query_gain, cosine_table, sine_table).astype(BF16)
    inv_key = inverse_rms(key_raw)
    hat_key = key_raw * inv_key
    key_rot = rotate(hat_key * key_gain, cosine_table, sine_table).astype(BF16)
    if split_tokens:
        keys_all = lax.all_gather(key_rot, W, axis=0, tiled=True)
        values_all = lax.all_gather(value_heads, W, axis=0, tiled=True)
    else:
        keys_all, values_all = key_rot, value_heads

    text_heads = (slot_count, local_heads, head_size)
    text_raw = dot(text_proj, text_slice)
    tkey_raw = text_raw[:, :head_width].reshape(text_heads)
    inv_tkey = inverse_rms(tkey_raw)
    hat_tkey = tkey_raw * inv_tkey
    text_key = (hat_tkey * textkey_gain).astype(BF16)
    text_value = text_raw[:, head_width:].astype(BF16).reshape(text_heads)
    keep_mask = (jnp.arange(slot_count) < caption_lengths[clip_index]).astype(F32)

    def scores_of(left, right):
        return jnp.einsum("thd,khd->htk", left, right, preferred_element_type=F32)

    def gather_of(weights, right):
        return jnp.einsum("htk,khd->thd", weights, right, preferred_element_type=F32)

    def scatter_of(weights, left):
        return jnp.einsum("htk,thd->khd", weights, left, preferred_element_type=F32)

    own_wts = jnp.exp(scores_of(query_rot, keys_all) * score_scale - score_shift)
    denom = jnp.sum(own_wts, axis=-1)
    own_out = gather_of(own_wts.astype(BF16), values_all) / denom.T[:, :, None]
    cross_wts = jnp.exp(scores_of(query_rot, text_key) * score_scale - score_shift) * keep_mask
    text_denom = jnp.sum(cross_wts, axis=-1)
    cross_out = gather_of(cross_wts.astype(BF16), text_value) / text_denom.T[:, :, None]
    text_gate = pick(jnp.tanh(cross_gate).reshape(tp_count, local_heads), tp_index)
    mixed = (own_out + text_gate[None, :, None] * cross_out).astype(BF16)

    mixed_parts = turn(mixed.reshape(tp_count, own_rows, head_width), tp)
    mixed_own = mixed_parts.transpose(1, 0, 2).reshape(own_rows, model_width)
    attn_out = dot(mixed_own, output_full)
    resid = token_float + gate_attn * attn_out
    inv_feed = inverse_rms(resid)
    hat_feed = resid * inv_feed
    normed_feed = hat_feed * feedforward_gain
    mod_own = (normed_feed * (1.0 + scale_feed) + shift_feed).astype(BF16)
    mod_ff = spread(mod_own, tp, masks).reshape(group_rows, model_width)

    hidden_pre = dot(mod_ff, hidden_slice)
    gate_pre, up_pre = hidden_pre[:, :local_hidden], hidden_pre[:, local_hidden:]
    sigmoid_gate = jax.nn.sigmoid(gate_pre)
    silu_gate = gate_pre * sigmoid_gate
    inner = (silu_gate * up_pre).astype(BF16)
    dfeed = (gate_feed * cotangent_all.astype(F32)).astype(BF16)
    dinner = dot(dfeed, down_slice, 1, 1)
    dgate_pre = (dinner * up_pre * (sigmoid_gate * (1.0 + gate_pre * (1.0 - sigmoid_gate)))).astype(BF16)
    dup_pre = (dinner * silu_gate).astype(BF16)
    dhidden = jnp.concatenate([dgate_pre, dup_pre], axis=1)
    dmod_parts = dot(dhidden, hidden_slice, 1, 1).reshape(tp_count, own_rows, model_width)
    dmod_ff = collect(dmod_parts, tp, masks)
    feed_parts = dot(inner, down_slice).reshape(tp_count, own_rows, model_width)
    feed_out = collect(feed_parts, tp, masks)

    def scatter_rows(grads):
        return lax.psum_scatter(grads.astype(BF16), dp, scatter_dimension=0, tiled=True)

    dhidden_rows = scatter_rows(dot(mod_ff, dhidden, 0, 0))
    downweight_grad = scatter_rows(dot(inner, dfeed, 0, 0)).astype(F32)

    block_output = resid + gate_feed * feed_out
    dout = cotangent[0].astype(F32)
    dgate_feed = jnp.sum(dout * feed_out, axis=0)
    dshift_feed = jnp.sum(dmod_ff, axis=0)
    dscale_feed = jnp.sum(dmod_ff * normed_feed, axis=0)
    dfeed_gain, dresid_norm = norm_backward(
        hat_feed, inv_feed, feedforward_gain, dmod_ff * (1.0 + scale_feed)
    )
    dresid = dout + dresid_norm
    dgate_attn = jnp.sum(dresid * attn_out, axis=0)
    dattn = (gate_attn * dresid).astype(BF16)

    dmixed_own = dot(dattn, output_full, 1, 1).astype(BF16)
    dmixed_parts = dmixed_own.reshape(own_rows, tp_count, head_width).transpose(1, 0, 2)
    dmixed = turn(dmixed_parts, tp).reshape(heads_shape).astype(F32)
    dout_parts = dot(mixed_own, dattn, 0, 0).reshape(dp_count, tp_count, weight_rows, model_width)
    dout_group = collect(
        dout_parts.transpose(1, 0, 2, 3).reshape(tp_count, dp_count * weight_rows, model_width), tp, masks
    )
    outweight_grad = clip_rows(
        dout_group.astype(BF16).reshape(dp_count, weight_rows, model_width), dp
    ).astype(F32)

    dcross_out = dmixed * text_gate[None, :, None]
    dcross_gate = jnp.sum(dmixed * cross_out, axis=(0, 2)) * (1.0 - text_gate * text_gate)
    dlevel_cross = -jnp.sum(dcross_out * cross_out, axis=-1) / text_denom.T
    dnumer_cross = (dcross_out / text_denom.T[:, :, None]).astype(BF16)
    cross_dscores = (
        cross_wts * (scores_of(dnumer_cross, text_value) + dlevel_cross.T[:, :, None])
    ).astype(BF16)
    dquery_cross = gather_of(cross_dscores, text_key)
    dtext_keys = scatter_of(cross_dscores, query_rot) * score_scale
    dtext_values = scatter_of(cross_wts.astype(BF16), dnumer_cross)
    if split_tokens:
        dtext_keys = lax.psum(dtext_keys, W)
        dtext_values = lax.psum(dtext_values, W)
    dtkey_gain, dtkey_raw = norm_backward(hat_tkey, inv_tkey, textkey_gain, dtext_keys)
    dtext_heads = jnp.concatenate(
        [
            dtkey_raw.astype(BF16).reshape(slot_count, head_width),
            dtext_values.astype(BF16).reshape(slot_count, head_width),
        ],
        axis=1,
    )
    dtext_group = collect(
        dot(dtext_heads, text_slice, 1, 1).reshape(tp_count, slot_part, model_width), tp, masks
    ).astype(BF16)
    dtext_clips = clip_spread(dtext_group, (C,)).reshape(clip_count * slot_part, model_width)
    dtext_all = (
        spread(dtext_clips, tp, masks)
        .reshape(tp_count, clip_count, slot_part, model_width)
        .transpose(1, 0, 2, 3)
        .reshape(clip_count * slot_count, model_width)
    )
    textweight_grad = dot(caption_columns, dtext_all, 0, 0)
    dcaption_parts = (
        dot(dtext_all, text_weight, 1, 1).astype(BF16).reshape(-1, caption_rows, text_rows)
    )
    dcaption_own = turn(dcaption_parts, (C, N))
    dcaption_wide = lax.all_gather(dcaption_own, W, axis=0, tiled=False)
    captions_grad = (
        dcaption_wide.reshape(wide_count, clip_count, narrow_count, caption_rows, text_rows)
        .transpose(3, 1, 0, 2, 4)
        .reshape(caption_rows, text_width)
        .astype(F32)
    )

    dlevel_self = -jnp.sum(dmixed * own_out, axis=-1) / denom.T
    dnumer_self = (dmixed / denom.T[:, :, None]).astype(BF16)
    dscores = (own_wts * (scores_of(dnumer_self, values_all) + dlevel_self.T[:, :, None])).astype(BF16)
    dquery_self = gather_of(dscores, keys_all)
    dkey = scatter_of(dscores, query_rot) * score_scale
    dvalue = scatter_of(own_wts.astype(BF16), dnumer_self)
    if split_tokens:
        dkey = lax.psum_scatter(dkey.astype(BF16), W, scatter_dimension=0, tiled=True).astype(F32)
        dvalue = lax.psum_scatter(dvalue.astype(BF16), W, scatter_dimension=0, tiled=True)
    dquery = rotate((dquery_self + dquery_cross) * score_scale, cosine_table, -sine_table)
    dquery_gain, dquery_raw = norm_backward(hat_query, inv_query, query_gain, dquery)
    dkey_gain, dkey_raw = norm_backward(hat_key, inv_key, key_gain, rotate(dkey, cosine_table, -sine_table))
    dqkv = jnp.concatenate(
        [x.astype(BF16).reshape(group_rows, head_width) for x in (dquery_raw, dkey_raw, dvalue)], axis=1
    )
    dmod_in = collect(dot(dqkv, qkv_slice, 1, 1).reshape(tp_count, own_rows, model_width), tp, masks)
    shared = 1.0 / wide_count if split_tokens else 1.0
    dhead_rows = scatter_rows(
        jnp.concatenate([dot(mod_in, dqkv, 0, 0), dot(text_proj, dtext_heads, 0, 0) * shared], axis=1)
    )

    dhead_parts = turn(dhead_rows.reshape(tp_count, weight_rows, 5 * head_width), tp)
    dhead_split = dhead_parts.reshape(tp_count, weight_rows, 5, head_width).transpose(2, 1, 0, 3)
    head_grads = dhead_split.reshape(5, weight_rows, model_width).astype(F32)
    dhidden_parts = turn(dhidden_rows.reshape(tp_count, weight_rows, 2 * local_hidden), tp)
    hidden_grads = (
        dhidden_parts.reshape(tp_count, weight_rows, 2, dp_count, hidden_rows)
        .transpose(2, 1, 3, 0, 4)
        .reshape(2, weight_rows, hidden_width)
        .astype(F32)
    )

    dshift_attn = jnp.sum(dmod_in, axis=0)
    dscale_attn = jnp.sum(dmod_in * normed_attn, axis=0)
    dattn_gain, dtokens_norm = norm_backward(
        hat_attn, inv_attn, attention_gain, dmod_in * (1.0 + scale_attn)
    )
    tokens_grad = dresid + dtokens_norm

    dgate_rows = jnp.zeros((tp_count, local_heads), F32)
    dgate_rows = lax.dynamic_update_index_in_dim(dgate_rows, dcross_gate, tp_index, 0).reshape(-1)
    pad = -head_count % head_size
    small = jnp.concatenate(
        [
            dshift_attn,
            dscale_attn,
            dgate_attn,
            dshift_feed,
            dscale_feed,
            dgate_feed,
            dattn_gain,
            dfeed_gain,
            dquery_gain,
            dkey_gain,
            dtkey_gain * shared,
            dgate_rows,
            jnp.zeros((pad,), F32),
        ]
    )
    clip_small = clip_spread(small_sum(small, PLANE), (C,))
    mod_width = 6 * model_width
    dmod_all = clip_small[:, :mod_width]
    gains = jnp.sum(clip_small[:, mod_width:], axis=0)
    attngain_grad, feedgain_grad = gains[:model_width], gains[model_width : 2 * model_width]
    rest = gains[2 * model_width :]
    querygain_grad, keygain_grad, textgain_grad = (
        rest[:head_size],
        rest[head_size : 2 * head_size],
        rest[2 * head_size : 3 * head_size],
    )
    crossgate_grad = rest[3 * head_size : 3 * head_size + head_count]
    modweight_grad = jnp.dot(cond_act.T, dmod_all, precision=HIGHEST, preferred_element_type=F32)
    dcond_act = jnp.dot(dmod_all, weight_float.T, precision=HIGHEST, preferred_element_type=F32)
    sigmoid_cond = jax.nn.sigmoid(cond_float)
    conditioning_grad = dcond_act * sigmoid_cond * (1.0 + cond_float * (1.0 - sigmoid_cond))
    modbias_grad = jnp.sum(dmod_all, axis=0)
    return (
        block_output[None],
        tokens_grad[None],
        captions_grad[None],
        conditioning_grad,
        modweight_grad,
        modbias_grad,
        attngain_grad,
        head_grads[0],
        head_grads[1],
        head_grads[2],
        querygain_grad,
        keygain_grad,
        textweight_grad,
        head_grads[3],
        head_grads[4],
        textgain_grad,
        crossgate_grad,
        outweight_grad,
        feedgain_grad,
        hidden_grads[0],
        hidden_grads[1],
        downweight_grad,
    )


def solution(mesh):
    rows, whole = P(ALL, None), P()
    tokens, captions = P(C, PLANE, None), P(C, N, None)
    columns = P(None, ALL)
    return jax.shard_map(
        on_device,
        mesh=mesh,
        in_specs=(
            tokens,
            P(C, PLANE),
            captions,
            whole,
            columns,
            rows,
            whole,
            whole,
            rows,
            rows,
            rows,
            whole,
            whole,
            rows,
            rows,
            rows,
            whole,
            whole,
            rows,
            whole,
            rows,
            rows,
            rows,
            tokens,
        ),
        out_specs=(
            tokens,
            tokens,
            captions,
            columns,
            rows,
            whole,
            whole,
            rows,
            rows,
            rows,
            whole,
            whole,
            rows,
            rows,
            rows,
            whole,
            whole,
            rows,
            whole,
            rows,
            rows,
            rows,
        ),
        check_vma=False,
    )
```

profile of v0, /device:TPU:0, one launch (start us, length us, event | category | flops | bytes accessed | tf_op | source)
XLA Modules:
  0.0 666.0 jit_solution(17494993792550547089)
XLA Ops:
  10.4 5.2 all-to-all-start.2
  16.7 5.7 all-to-all-done.2
  24.2 12.0 %all_to_all.45 = bf16[8,48,576]{2,1,0:T(8,128)(2,1)} all-to-all(bf16[8,48,576]{2,1,0:T(8,128)(2,1)S(1)} %pad_maximum_fusion.12), channel_id=1, replica_groups=mesh['clip'=4,'wide'=4,'narrow'=2] {'wide','narrow'}, dimensions={0} | all-to-all | bytes 884736 | tf_op jit(solution)/shard_map/all_to_all | solution.py:150
  37.2 15.2 %all_to_all.46 = bf16[8,48,1024]{2,1,0:T(8,128)(2,1)} all-to-all(bf16[8,48,1024]{2,1,0:T(8,128)(2,1)S(1)} %pad_maximum_fusion.5), channel_id=1, replica_groups=mesh['clip'=4,'wide'=4,'narrow'=2] {'wide','narrow'}, dimensions={0} | all-to-all | bytes 1572864 | tf_op jit(solution)/shard_map/all_to_all | solution.py:150
  94.0 8.8 %collective-permute-done.11 = bf16[128,1536]{1,0:T(8,128)(2,1)S(1)} collective-permute-done((bf16[128,1536]{1,0:T(8,128)(2,1)S(1)}, bf16[128,1536]{1,0:T(8,128)(2,1)S(1)}, u32[]{:S(2)}, u32[]{:S(2)}) %collective-permute-start.11) | collective-permute-done | bytes 393248 | tf_op jit(solution)/shard_map/ppermute | solution.py:59
  154.7 4.8 fusion.6
  161.9 4.8 collective-permute-done.36
  231.1 4.9 copy.253
  250.3 5.6 collective-permute-done.55
  267.4 8.3 %fusion.171 = f32[1024,1024]{0,1:T(8,128)} fusion(bf16[1024,1536]{1,0:T(8,128)(2,1)} %bitcast.94, bf16[1536,1024]{1,0:T(8,128)(2,1)} %all-gather.11.cloned.1.call-done), kind=kOutput, calls=%fused_computation.459 | convolution fusion | flops 3221225472 | bytes 10485760 | tf_op jit(solution)/shard_map/dot_general | solution.py:18
  275.7 6.2 multiply_convert_fusion.3
  303.4 4.9 bitcast_add_fusion.11
  318.3 5.4 collective-permute-done.69
  328.9 4.8 collective-permute-done.88
  348.4 7.7 %convolution_convert_fusion = bf16[1536,1024]{1,0:T(8,128)(2,1)} fusion(bf16[1024,1536]{1,0:T(8,128)(2,1)} %bitcast.94, bf16[1024,512]{0,1:T(8,128)(2,1)} %copy-done.145, bf16[1024,512]{0,1:T(8,128)(2,1)} %copy-done.144), kind=kOutput, calls=%fused_computation.14 | convolution fusion | flops 3226992640 | bytes 8388608 | tf_op jit(solution)/shard_map/dot_general | solution.py:18
  365.9 7.1 %multiply_convert_fusion = bf16[3,1024,1024]{1,2,0:T(8,128)(2,1)S(1)} fusion(f32[3,1024,1024]{1,2,0:T(8,128)} %copy-done.1, f32[3,1024]{1,0:T(4,128)S(1)} %bitcast_divide_fusion.1, bf16[1024,3,64]{0,2,1:T(8,128)(2,1)S(1)} %bitcast.553, f32[1024,3,64]{0,2,1:T(8,128)S(1)} %reshape.584, f32[1024,3]{0,1:T(4,128)S(1)} %bitcast.595), kind=kOutput, calls=%fused_computation | convolution fusion | flops 418775040 | bytes 20078592 | tf_op jit(solution)/shard_map/thd,khd->htk/dot_general | solution.py:296
  402.1 5.3 convolution_convert_fusion.2
  475.9 8.4 %collective-permute-start.110 = (bf16[32,1536]{1,0:T(8,128)(2,1)S(1)}, bf16[32,1536]{1,0:T(8,128)(2,1)S(1)}, u32[]{:S(2)}, u32[]{:S(2)}) collective-permute-start(bf16[32,1536]{1,0:T(8,128)(2,1)S(1)} %pad_maximum_fusion.22), channel_id=1, source_target_pairs={{0,8},{8,0},{16,24},{24,16},{1,9},{9,1},{17,25},{25,17},{2,10},{10... | collective-permute-start | bytes 294920 | tf_op jit(solution)/shard_map/ppermute | solution.py:59
  489.3 7.3 %collective-permute-done.111 = bf16[32,1536]{1,0:T(8,128)(2,1)S(1)} collective-permute-done((bf16[32,1536]{1,0:T(8,128)(2,1)S(1)}, bf16[32,1536]{1,0:T(8,128)(2,1)S(1)}, u32[]{:S(2)}, u32[]{:S(2)}) %collective-permute-start.111) | collective-permute-done | bytes 98336 | tf_op jit(solution)/shard_map/ppermute | solution.py:59
  497.9 7.8 %collective-permute-done.112 = bf16[32,1536]{1,0:T(8,128)(2,1)S(1)} collective-permute-done((bf16[32,1536]{1,0:T(8,128)(2,1)S(1)}, bf16[32,1536]{1,0:T(8,128)(2,1)S(1)}, u32[]{:S(2)}, u32[]{:S(2)}) %collective-permute-start.112) | collective-permute-done | bytes 98336 | tf_op jit(solution)/shard_map/ppermute | solution.py:59
  519.7 6.5 collective-permute-done.97
  526.9 11.0 %collective-permute-done.95 = bf16[64,1536]{1,0:T(8,128)(2,1)S(1)} collective-permute-done((bf16[64,1536]{1,0:T(8,128)(2,1)S(1)}, bf16[64,1536]{1,0:T(8,128)(2,1)S(1)}, u32[]{:S(2)}, u32[]{:S(2)}) %collective-permute-start.95) | collective-permute-done | bytes 196640 | tf_op jit(solution)/shard_map/ppermute | solution.py:59
  609.9 13.0 %all-to-all-done.8 = bf16[8,48,1024]{2,1,0:T(8,128)(2,1)S(1)} async-done(((bf16[8,48,1024]{2,1,0:T(8,128)(2,1)}), bf16[8,48,1024]{2,1,0:T(8,128)(2,1)S(1)}, u32[]{:S(2)}, u32[]{:S(2)}) %all-to-all-start.8) | async-done | bytes 786464 | tf_op jit(solution)/shard_map/all_to_all | solution.py:150
  645.6 7.9 %fusion.156 = (f32[1,48,8,192]{3,0,1,2:T(1,128)S(1)}, f32[1,48,8,192]{3,0,1,2:T(1,128)S(1)}, f32[1,48,8,192]{3,0,1,2:T(1,128)S(1)}, f32[1,48,8,192]{3,0,1,2:T(1,128)S(1)}, f32[1,48,8,192]{3,0,1,2:T(1,128)S(1)}) fusion(f32[5,48,8,192]{3,0,1,2:T(8,128)} %bitcast.530), kind=kLoop, calls=%fused_computation.444 | loop fusion | bytes 2949120 | tf_op jit(solution)/shard_map/slice | solution.py:502
  (950 shorter events, 470.2 us)
Async XLA Ops:
  15.6 163.0 %all-gather.9.cloned.1.call-start = ((), (), s32[]{:S(2)}) async-start(), calls=%async_computation.13 | async-start | bytes 2211840 | tf_op jit(solution)/shard_map/all_gather | solution.py:214
  23.2 167.7 %all-gather.7.cloned.1.call-start = ((), (), s32[]{:S(2)}) async-start(), calls=%async_computation.12 | async-start | bytes 2457600 | tf_op jit(solution)/shard_map/all_gather | solution.py:214
  36.2 231.2 %all-gather.11.cloned.1.call-start = ((), (), s32[]{:S(2)}) async-start(), calls=%async_computation.14 | async-start | bytes 3932160 | tf_op jit(solution)/shard_map/all_gather | solution.py:214
  54.1 25.5 %collective-permute-start.21 = (s32[1,128]{1,0:T(1,128)S(1)}, s32[1,128]{1,0:T(1,128)S(1)}, u32[]{:S(2)}, u32[]{:S(2)}) collective-permute-start(s32[1,128]{1,0:T(1,128)S(1)} %copy-done.141), channel_id=1, source_target_pairs={{0,2},{1,3},{2,0},{3,1},{4,6},{5,7},{6,4},{7,5},{8,10},{9,11},{10,... | collective-permute-start | bytes 1544 | tf_op jit(solution)/shard_map/ppermute | solution.py:59
  54.6 26.3 %collective-permute-start = (f32[9216]{0:T(1024)S(1)}, f32[9216]{0:T(1024)S(1)}, u32[]{:S(2)}, u32[]{:S(2)}) collective-permute-start(f32[9216]{0:T(1024)S(1)} %bitcast.607), channel_id=1, source_target_pairs={{0,8},{8,0},{16,24},{24,16},{1,9},{9,1},{17,25},{25,17},{2,10},{10... | collective-permute-start | bytes 110600 | tf_op jit(solution)/shard_map/ppermute | solution.py:59
  60.4 54.2 %all-to-all-start.1 = ((bf16[8,128,128]{2,1,0:T(8,128)(2,1)}), bf16[8,128,128]{2,1,0:T(8,128)(2,1)S(1)}, u32[]{:S(2)}, u32[]{:S(2)}) async-start(bf16[8,128,128]{2,1,0:T(8,128)(2,1)} %bitcast.36), calls=%async_computation.1 | async-start | bytes 524288 | tf_op jit(solution)/shard_map/all_to_all | solution.py:150
  63.8 211.9 %all-gather.13.cloned.1.call-start = ((), (), s32[]{:S(2)}) async-start(), calls=%async_computation.15 | async-start | bytes 1966080 | tf_op jit(solution)/shard_map/all_gather | solution.py:214
  92.2 32.7 %collective-permute-start.14 = (bf16[128,1536]{1,0:T(8,128)(2,1)S(1)}, bf16[128,1536]{1,0:T(8,128)(2,1)}, u32[]{:S(2)}, u32[]{:S(2)}) collective-permute-start(bf16[128,1536]{1,0:T(8,128)(2,1)S(1)} %bitcast.536), channel_id=1, source_target_pairs={{0,2},{1,3},{2,0},{3,1},{4,6},{5,7},{6,4},{7,5},{8,10},{9,11},{10,... | collective-permute-start | bytes 1179656 | tf_op jit(solution)/shard_map/ppermute | solution.py:59
  133.1 36.8 %collective-permute-start.79 = (bf16[128,1536]{1,0:T(8,128)(2,1)S(1)}, bf16[128,1536]{1,0:T(8,128)(2,1)S(1)}, u32[]{:S(2)}, u32[]{:S(2)}) collective-permute-start(bf16[128,1536]{1,0:T(8,128)(2,1)S(1)} %constant_dynamic-update-slice_fusion.19), channel_id=1, source_target_pairs={{0,2},{1,3},{2,0},{3,1},{4,6},{5,7},{6,4},{7,5},{8,10},{9,11},{10,... | collective-permute-start | bytes 1179656 | tf_op jit(solution)/shard_map/ppermute | solution.py:59
  185.2 29.6 %collective-permute-start.46 = (bf16[192,1536]{1,0:T(8,128)(2,1)}, bf16[192,1536]{1,0:T(8,128)(2,1)}, u32[]{:S(2)}, u32[]{:S(2)}) collective-permute-start(bf16[192,1536]{1,0:T(8,128)(2,1)} %reshape.554), channel_id=1, source_target_pairs={{0,1},{1,0},{2,3},{3,2},{4,5},{5,4},{6,7},{7,6},{8,9},{9,8},{10,11... | collective-permute-start | bytes 1769480 | tf_op jit(solution)/shard_map/ppermute | solution.py:59
  187.3 39.3 %collective-permute-start.50 = (bf16[192,1536]{1,0:T(8,128)(2,1)}, bf16[192,1536]{1,0:T(8,128)(2,1)}, u32[]{:S(2)}, u32[]{:S(2)}) collective-permute-start(bf16[192,1536]{1,0:T(8,128)(2,1)} %reshape.554), channel_id=1, source_target_pairs={{0,2},{1,3},{2,0},{3,1},{4,6},{5,7},{6,4},{7,5},{8,10},{9,11},{10,... | collective-permute-start | bytes 1769480 | tf_op jit(solution)/shard_map/ppermute | solution.py:59
  208.1 27.9 %all-to-all-start.3 = ((bf16[8,128,192]{1,2,0:T(8,128)(2,1)}), bf16[8,128,192]{1,2,0:T(8,128)(2,1)S(1)}, u32[]{:S(2)}, u32[]{:S(2)}) async-start(bf16[8,128,192]{1,2,0:T(8,128)(2,1)} %copy.252), calls=%async_computation.3 | async-start | bytes 786432 | tf_op jit(solution)/shard_map/all_to_all | solution.py:150
  348.4 255.3 %reduce-scatter.6.cloned.1.call-start = ((), (), s32[]{:S(2)}) async-start(), calls=%async_computation.16 | async-start | bytes 3932160 | tf_op jit(solution)/shard_map/reduce_scatter | solution.py:339
  356.1 266.8 %reduce-scatter.10.cloned.1.call-start = ((), (), s32[]{:S(2)}) async-start(), calls=%async_computation.19 | async-start | bytes 3932160 | tf_op jit(solution)/shard_map/reduce_scatter | solution.py:339
  393.6 237.1 %reduce-scatter.8.cloned.1.call-start = ((), (), s32[]{:S(2)}) async-start(), calls=%async_computation.17 | async-start | bytes 1966080 | tf_op jit(solution)/shard_map/reduce_scatter | solution.py:339
  417.3 56.1 %collective-permute-start.131 = (bf16[192,1536]{1,0:T(8,128)(2,1)}, bf16[192,1536]{1,0:T(8,128)(2,1)}, u32[]{:S(2)}, u32[]{:S(2)}) collective-permute-start(bf16[192,1536]{1,0:T(8,128)(2,1)} %get-tuple-element.56), channel_id=1, source_target_pairs={{0,2},{1,3},{2,0},{3,1},{4,6},{5,7},{6,4},{7,5},{8,10},{9,11},{10,... | collective-permute-start | bytes 1769480 | tf_op jit(solution)/shard_map/ppermute | solution.py:59
  472.0 37.0 %collective-permute-start.90 = (bf16[128,1536]{1,0:T(8,128)(2,1)S(1)}, bf16[128,1536]{1,0:T(8,128)(2,1)S(1)}, u32[]{:S(2)}, u32[]{:S(2)}) collective-permute-start(bf16[128,1536]{1,0:T(8,128)(2,1)S(1)} %copy-done.78), channel_id=1, source_target_pairs={{0,2},{1,3},{2,0},{3,1},{4,6},{5,7},{6,4},{7,5},{8,10},{9,11},{10,... | collective-permute-start | bytes 1179656 | tf_op jit(solution)/shard_map/ppermute | solution.py:59
  473.5 35.5 %collective-permute-start.91 = (bf16[128,1536]{1,0:T(8,128)(2,1)}, bf16[128,1536]{1,0:T(8,128)(2,1)S(1)}, u32[]{:S(2)}, u32[]{:S(2)}) collective-permute-start(bf16[128,1536]{1,0:T(8,128)(2,1)} %get-tuple-element.64), channel_id=1, source_target_pairs={{0,2},{1,3},{2,0},{3,1},{4,6},{5,7},{6,4},{7,5},{8,10},{9,11},{10,... | collective-permute-start | bytes 1179656 | tf_op jit(solution)/shard_map/ppermute | solution.py:59
  473.7 37.4 %collective-permute-start.93 = (bf16[128,1536]{1,0:T(8,128)(2,1)}, bf16[128,1536]{1,0:T(8,128)(2,1)S(1)}, u32[]{:S(2)}, u32[]{:S(2)}) collective-permute-start(bf16[128,1536]{1,0:T(8,128)(2,1)} %get-tuple-element.63), channel_id=1, source_target_pairs={{0,2},{1,3},{2,0},{3,1},{4,6},{5,7},{6,4},{7,5},{8,10},{9,11},{10,... | collective-permute-start | bytes 1179656 | tf_op jit(solution)/shard_map/ppermute | solution.py:59
  475.1 37.5 %collective-permute-start.94 = (bf16[128,1536]{1,0:T(8,128)(2,1)}, bf16[128,1536]{1,0:T(8,128)(2,1)S(1)}, u32[]{:S(2)}, u32[]{:S(2)}) collective-permute-start(bf16[128,1536]{1,0:T(8,128)(2,1)} %get-tuple-element.62), channel_id=1, source_target_pairs={{0,2},{1,3},{2,0},{3,1},{4,6},{5,7},{6,4},{7,5},{8,10},{9,11},{10,... | collective-permute-start | bytes 1179656 | tf_op jit(solution)/shard_map/ppermute | solution.py:59
  509.0 45.2 %collective-permute-start.133 = (bf16[96,1536]{1,0:T(8,128)(2,1)}, bf16[96,1536]{1,0:T(8,128)(2,1)}, u32[]{:S(2)}, u32[]{:S(2)}) collective-permute-start(bf16[96,1536]{1,0:T(8,128)(2,1)} %slice.630), channel_id=1, source_target_pairs={{0,1},{1,0},{2,3},{3,2},{4,5},{5,4},{6,7},{7,6},{8,9},{9,8},{10,11... | collective-permute-start | bytes 884744 | tf_op jit(solution)/shard_map/ppermute | solution.py:59
  511.0 29.9 %collective-permute-start.114 = (bf16[128,1536]{1,0:T(8,128)(2,1)S(1)}, bf16[128,1536]{1,0:T(8,128)(2,1)S(1)}, u32[]{:S(2)}, u32[]{:S(2)}) collective-permute-start(bf16[128,1536]{1,0:T(8,128)(2,1)S(1)} %bitcast.574), channel_id=1, source_target_pairs={{0,4},{1,5},{2,6},{3,7},{4,0},{5,1},{6,2},{7,3},{8,12},{9,13},{10,... | collective-permute-start | bytes 1179656 | tf_op jit(solution)/shard_map/ppermute | solution.py:59
  512.6 27.0 %collective-permute-start.113 = (bf16[128,1536]{1,0:T(8,128)(2,1)S(1)}, bf16[128,1536]{1,0:T(8,128)(2,1)S(1)}, u32[]{:S(2)}, u32[]{:S(2)}) collective-permute-start(bf16[128,1536]{1,0:T(8,128)(2,1)S(1)} %bitcast.575), channel_id=1, source_target_pairs={{0,1},{1,0},{2,3},{3,2},{4,5},{5,4},{6,7},{7,6},{8,9},{9,8},{10,11... | collective-permute-start | bytes 1179656 | tf_op jit(solution)/shard_map/ppermute | solution.py:59
  588.9 43.8 %all-gather.15.cloned.1.call-start = ((), (), s32[]{:S(2)}) async-start(), calls=%async_computation.18 | async-start | bytes 1310720 | tf_op jit(solution)/shard_map/all_gather | solution.py:403
  (288 other events, 2592.6 us)
Sparse Core Ops, SparseCore 0:
  23.4 41.7 all-gather.8
  66.7 43.6 all-gather.6
  111.9 70.7 all-gather.10
  184.2 35.6 all-gather.12
  356.3 66.7 reduce-scatter.5
  425.2 60.2 reduce-scatter.9
  487.9 39.2 reduce-scatter.7
  601.0 24.8 all-gather.14
where the time goes:
time: 672 us; the launch traced here: 666 us
  local copies, waits for them, and re-layouts  190 us (28%)
  starting transfers between devices  149 us (22%)
  waiting for transfers between devices  131 us (19%)
  matrix products  88.9 us (13%)
  other arithmetic  62.8 us (9%)
  blocking collectives  27.2 us (4%)
  between operations  17.3 us (3%)
    ppermute x144, starting transfers between devices, swap(): lax.ppermute(x, axes, [(i, i ^ mask) for i in range(axes_size(axes))])  120 us
    ppermute x144, waiting for transfers between devices, swap(): lax.ppermute(x, axes, [(i, i ^ mask) for i in range(axes_size(axes))])  112 us
    dot_general x18, matrix products, dot(): lax.dot_general(left, right, (((left_dim,), (right_dim,)), ((), ())), pre...  60.2 us
    dynamic_update_slice x54, local copies, waits for them, and re-layouts, spread(): out = lax.dynamic_update_index_in_dim(out, piece, me ^ mask, 0)  36.7 us
    unnamed x317, local copies, waits for them, and re-layouts  28.9 us
    all_to_all x2, blocking collectives, turn(): return lax.all_to_all(x, axes, split_axis=0, concat_axis=0, tiled=False)  27.2 us
    all_to_all x7, starting transfers between devices, turn(): return lax.all_to_all(x, axes, split_axis=0, concat_axis=0, tiled=False)  27 us
    all_to_all x7, waiting for transfers between devices, turn(): return lax.all_to_all(x, axes, split_axis=0, concat_axis=0, tiled=False)  18.7 us
  transfers between devices with their start and end apart: 159, of which 44 were waited for; matrix products, arithmetic and copies ran while one was open for 42% of the time, Pallas kernels for 0%

commit v1 on v0

v1 whole, which is shorter than its diff:
```python
import functools
import math

import jax
import jax.numpy as jnp
from jax import lax
from jax.experimental import pallas as pl
from jax.experimental.pallas import tpu as pltpu
from jax.sharding import PartitionSpec as P

EPSILON = 1e-06
ROPE_BASE = 10000.0
C, W, N = "clip", "wide", "narrow"
ALL = (C, W, N)
PLANE = (W, N)
BF16, F32 = jnp.bfloat16, jnp.float32
HIGHEST = lax.Precision.HIGHEST


def dot(left, right, left_dim=1, right_dim=0):
    return lax.dot_general(
        left, right, (((left_dim,), (right_dim,)), ((), ())), preferred_element_type=F32
    )


def inverse_rms(values):
    return lax.rsqrt(jnp.mean(values * values, axis=-1, keepdims=True) + EPSILON)


def norm_backward(normed, inv_scale, gain, upstream):
    gain_grad = jnp.sum((upstream * normed).reshape(-1, normed.shape[-1]), axis=0)
    scaled = upstream * gain
    values_grad = inv_scale * (scaled - normed * jnp.mean(scaled * normed, axis=-1, keepdims=True))
    return (gain_grad, values_grad)


def rope_tables(positions, head_size):
    half_size = head_size // 2
    frequency = jnp.exp(-math.log(ROPE_BASE) * 2.0 * jnp.arange(half_size, dtype=F32) / head_size)
    angles = positions.astype(F32)[:, None] * frequency[None, :]
    cosine, sine = jnp.cos(angles), jnp.sin(angles)
    return (jnp.concatenate([cosine, cosine], axis=1), jnp.concatenate([-sine, sine], axis=1))


def swap_halves(values):
    half_size = values.shape[1] // 2
    return jnp.concatenate([values[:, half_size:], values[:, :half_size]], axis=1)


def full_spec(shape):
    return pl.BlockSpec(shape, lambda *_: (0,) * len(shape))


def row_spec(rows, width):
    return pl.BlockSpec((rows, width), lambda i, *_: (i, 0))


def struct(shape, dtype):
    return jax.ShapeDtypeStruct(shape, dtype)


def head_parts(width, size):
    return [slice(at, at + size) for at in range(0, width, size)]


def prepare_body(raw_ref, cos_ref, sin_ref, query_gain_ref, key_gain_ref, query_ref, key_ref, value_ref):
    width, size = query_ref.shape[1], query_gain_ref.shape[1]
    raw, cosine, sine = raw_ref[...], cos_ref[...], sin_ref[...]
    for out_ref, gain, base in ((query_ref, query_gain_ref[...], 0), (key_ref, key_gain_ref[...], width)):
        heads = []
        for part in head_parts(width, size):
            head = raw[:, base + part.start : base + part.stop]
            head = head * inverse_rms(head) * gain
            heads.append(head * cosine + swap_halves(head) * sine)
        out_ref[...] = jnp.concatenate(heads, axis=1).astype(BF16)
    value_ref[...] = raw[:, 2 * width :].astype(BF16)


def prepare(raw, cosine, sine, query_gain, key_gain, width):
    rows, size = raw.shape[0], cosine.shape[1]
    block = math.gcd(rows, 256)
    return pl.pallas_call(
        prepare_body,
        grid=(rows // block,),
        in_specs=[
            row_spec(block, raw.shape[1]),
            row_spec(block, size),
            row_spec(block, size),
            full_spec((1, size)),
            full_spec((1, size)),
        ],
        out_specs=[row_spec(block, width)] * 3,
        out_shape=[struct((rows, width), BF16)] * 3,
        name="prepare",
    )(raw, cosine, sine, query_gain[None], key_gain[None])


def prepare_text_body(raw_ref, gain_ref, key_ref, value_ref):
    width, size = key_ref.shape[1], gain_ref.shape[1]
    raw, gain = raw_ref[...], gain_ref[...]
    heads = [raw[:, part] for part in head_parts(width, size)]
    heads = [head * inverse_rms(head) * gain for head in heads]
    key_ref[...] = jnp.concatenate(heads, axis=1).astype(BF16)
    value_ref[...] = raw[:, width:].astype(BF16)


def prepare_text(raw, gain, width):
    return pl.pallas_call(
        prepare_text_body, out_shape=[struct((raw.shape[0], width), BF16)] * 2, name="prepare_text"
    )(raw, gain[None])


def weights_of(left, right, factor, offset):
    scores = lax.dot_general(left, right, (((1,), (1,)), ((), ())), preferred_element_type=F32)
    return jnp.exp2(scores * factor - offset)


def attend_body(
    order_ref,
    query_ref,
    key_ref,
    value_ref,
    text_key_ref,
    text_value_ref,
    keep_ref,
    gate_ref,
    mixed_ref,
    own_ref,
    cross_ref,
    denom_ref,
    text_denom_ref,
    *,
    size,
    factor,
    offset,
):
    rows, width = query_ref.shape
    part_rows = mixed_ref.shape[1]
    keep = keep_ref[...]
    results = []
    for part in head_parts(width, size):
        query = query_ref[:, part]
        wts = weights_of(query, key_ref[:, part], factor, offset)
        denom = jnp.sum(wts, axis=1, keepdims=True)
        own = dot(wts.astype(BF16), value_ref[:, part]) / denom
        text_wts = weights_of(query, text_key_ref[:, part], factor, offset) * keep
        text_denom = jnp.sum(text_wts, axis=1, keepdims=True)
        cross = dot(text_wts.astype(BF16), text_value_ref[:, part]) / text_denom
        shape = (rows, size)
        results.append(
            (own, cross, jnp.broadcast_to(denom, shape), jnp.broadcast_to(text_denom, shape))
        )
    own, cross, denom, text_denom = (jnp.concatenate(heads, axis=1) for heads in zip(*results))
    own_ref[...], cross_ref[...], denom_ref[...], text_denom_ref[...] = own, cross, denom, text_denom
    mixed = (own + gate_ref[...] * cross).astype(BF16)
    first = pl.program_id(0) * (rows // part_rows)
    for index in range(rows // part_rows):
        mixed_ref[order_ref[first + index]] = mixed[index * part_rows : (index + 1) * part_rows]


def attend(order, query, keys, values, text_key, text_value, keep, gate, size):
    rows, width = query.shape
    slots = text_key.shape[0]
    part_rows = rows // order.shape[0]
    block = part_rows * math.gcd(order.shape[0], max(1, 256 // part_rows))
    body = functools.partial(
        attend_body, size=size, factor=size**-0.5 / math.log(2.0), offset=3.0 * size**0.5 / math.log(2.0)
    )
    return pl.pallas_call(
        body,
        grid_spec=pltpu.PrefetchScalarGridSpec(
            num_scalar_prefetch=1,
            grid=(rows // block,),
            in_specs=[
                row_spec(block, width),
                full_spec(keys.shape),
                full_spec(values.shape),
                full_spec((slots, width)),
                full_spec((slots, width)),
                full_spec((1, slots)),
                full_spec((1, width)),
            ],
            out_specs=[full_spec((order.shape[0], part_rows, width))] + [row_spec(block, width)] * 4,
        ),
        out_shape=[struct((order.shape[0], part_rows, width), BF16)] + [struct((rows, width), F32)] * 4,
        name="attend",
    )(order, query, keys, values, text_key, text_value, keep[None], gate[None])


def attend_back_body(
    order_ref, query_ref, out_ref, denom_ref, dmixed_ref, key_ref, value_ref, *refs, size, factor, offset, text
):
    if text:
        keep_ref, gate_ref, dquery_ref, dkey_ref, dvalue_ref, dgate_ref = refs
    else:
        start_ref, dquery_ref, dkey_ref, dvalue_ref = refs
    rows, width = query_ref.shape
    part_rows = dmixed_ref.shape[1]
    step = pl.program_id(0)
    first = step * (rows // part_rows)
    dmixed = jnp.concatenate(
        [dmixed_ref[order_ref[first + index]] for index in range(rows // part_rows)], axis=0
    ).astype(F32)
    out, inv = out_ref[...], 1.0 / denom_ref[...]

    @pl.when(step == 0)
    def _():
        dkey_ref[...] = jnp.zeros_like(dkey_ref)
        dvalue_ref[...] = jnp.zeros_like(dvalue_ref)
        if text:
            dgate_ref[...] = jnp.zeros_like(dgate_ref)

    if text:
        dgate_ref[...] += jnp.sum(dmixed * out, axis=0, keepdims=True)
        dmixed = dmixed * gate_ref[...]
    dnumer = (dmixed * inv).astype(BF16)
    level = -(dmixed * out * inv)
    scale = size**-0.5
    results = []
    for part in head_parts(width, size):
        query, keys, numer = query_ref[:, part], key_ref[:, part], dnumer[:, part]
        column = jnp.sum(level[:, part], axis=1, keepdims=True)
        level_row = jnp.broadcast_to(column, (rows, 128)).T[:1]
        wts = weights_of(keys, query, factor, offset)
        if text:
            wts = wts * keep_ref[...]
        dwts = lax.dot_general(
            value_ref[:, part], numer, (((1,), (1,)), ((), ())), preferred_element_type=F32
        )
        dscores = (wts * (dwts + level_row)).astype(BF16)
        dquery = (dot(keys.T, dscores) * scale).T
        results.append((dquery, dot(dscores, query) * scale, dot(wts.astype(BF16), numer)))
    dquery, dkey, dvalue = (jnp.concatenate(heads, axis=1) for heads in zip(*results))
    dquery_ref[...] = dquery if text else dquery + start_ref[...]
    dkey_ref[...] += dkey
    dvalue_ref[...] += dvalue


def attend_back(order, query, out, denom, dmixed, keys, values, size, text=None, start=None):
    rows, width = query.shape
    slots = keys.shape[0]
    part_rows = rows // order.shape[0]
    block = part_rows * math.gcd(order.shape[0], max(1, 256 // part_rows))
    body = functools.partial(
        attend_back_body,
        size=size,
        factor=size**-0.5 / math.log(2.0),
        offset=3.0 * size**0.5 / math.log(2.0),
        text=text is not None,
    )
    if text is None:
        extra, extra_specs = (start,), [row_spec(block, width)]
    else:
        extra, extra_specs = (text[0][:, None], text[1][None]), [full_spec((slots, 1)), full_spec((1, width))]
    ends = [] if text is None else [(1, width)]
    return pl.pallas_call(
        body,
        grid_spec=pltpu.PrefetchScalarGridSpec(
            num_scalar_prefetch=1,
            grid=(rows // block,),
            in_specs=[row_spec(block, width)] * 3
            + [full_spec(dmixed.shape), full_spec(keys.shape), full_spec(keys.shape)]
            + extra_specs,
            out_specs=[row_spec(block, width)]
            + [full_spec(keys.shape)] * 2
            + [full_spec(shape) for shape in ends],
        ),
        out_shape=[struct((rows, width), F32)]
        + [struct(keys.shape, F32)] * 2
        + [struct(shape, F32) for shape in ends],
        name="text_back" if text else "attend_back",
    )(order, query, out, denom, dmixed, keys, values, *extra)


def norm_heads_back(raw, upstream, gain, size):
    gain_grad, grads = 0.0, []
    for part in head_parts(raw.shape[1], size):
        head, grad = raw[:, part], upstream[part.start // size]
        inv = inverse_rms(head)
        hat = head * inv
        gain_grad = gain_grad + jnp.sum(grad * hat, axis=0, keepdims=True)
        scaled = grad * gain
        grads.append(inv * (scaled - hat * jnp.mean(scaled * hat, axis=1, keepdims=True)))
    return gain_grad, jnp.concatenate(grads, axis=1)


def finish_body(
    raw_ref, dquery_ref, dkey_ref, dvalue_ref, cos_ref, sin_ref, query_gain_ref, key_gain_ref, out_ref, gain_ref
):
    width, size = dquery_ref.shape[1], query_gain_ref.shape[1]
    cosine, sine = cos_ref[...], sin_ref[...]

    @pl.when(pl.program_id(0) == 0)
    def _():
        gain_ref[...] = jnp.zeros_like(gain_ref)

    gains, outs = [], []
    for grad_ref, gain, base in ((dquery_ref, query_gain_ref[...], 0), (dkey_ref, key_gain_ref[...], width)):
        upstream = []
        for part in head_parts(width, size):
            grad = grad_ref[:, part].astype(F32)
            upstream.append(grad * cosine - swap_halves(grad) * sine)
        gain_grad, grads = norm_heads_back(raw_ref[:, base : base + width], upstream, gain, size)
        gains.append(gain_grad)
        outs.append(grads.astype(BF16))
    out_ref[...] = jnp.concatenate(outs + [dvalue_ref[...].astype(BF16)], axis=1)
    gain_ref[...] += jnp.concatenate(gains, axis=0)


def finish(raw, dquery, dkey, dvalue, cosine, sine, query_gain, key_gain):
    rows, width = dquery.shape
    size = cosine.shape[1]
    block = math.gcd(rows, 256)
    return pl.pallas_call(
        finish_body,
        grid=(rows // block,),
        in_specs=[row_spec(block, 3 * width)]
        + [row_spec(block, width)] * 3
        + [row_spec(block, size)] * 2
        + [full_spec((1, size))] * 2,
        out_specs=[row_spec(block, 3 * width), full_spec((2, size))],
        out_shape=[struct((rows, 3 * width), BF16), struct((2, size), F32)],
        name="finish",
    )(raw, dquery, dkey, dvalue, cosine, sine, query_gain[None], key_gain[None])


def finish_text_body(raw_ref, dkey_ref, dvalue_ref, gain_in_ref, out_ref, gain_ref):
    width, size = dkey_ref.shape[1], gain_in_ref.shape[1]
    upstream = [dkey_ref[:, part] for part in head_parts(width, size)]
    gain_ref[...], grads = norm_heads_back(raw_ref[:, :width], upstream, gain_in_ref[...], size)
    out_ref[...] = jnp.concatenate([grads.astype(BF16), dvalue_ref[...].astype(BF16)], axis=1)


def finish_text(raw, dkey, dvalue, gain):
    return pl.pallas_call(
        finish_text_body,
        out_shape=[struct(raw.shape, BF16), struct((1, gain.shape[0]), F32)],
        name="finish_text",
    )(raw, dkey, dvalue, gain[None])


def join_body(parts_ref, *outs, width):
    for index, out_ref in enumerate(outs):
        for turn_index in range(parts_ref.shape[0]):
            at = turn_index * width
            out_ref[:, at : at + width] = parts_ref[turn_index, :, index * width : (index + 1) * width].astype(F32)


def join_heads(parts, width):
    count, rows, total = parts.shape
    return pl.pallas_call(
        functools.partial(join_body, width=width),
        out_shape=[struct((rows, count * width), F32)] * (total // width),
        name="join_heads",
    )(parts)


def join_hidden_body(parts_ref, gate_ref, up_ref, *, groups, width):
    count = parts_ref.shape[0]
    for index, out_ref in enumerate((gate_ref, up_ref)):
        for group in range(groups):
            for turn_index in range(count):
                at = (group * count + turn_index) * width
                source = (index * groups + group) * width
                out_ref[:, at : at + width] = parts_ref[turn_index, :, source : source + width].astype(F32)


def join_hidden(parts, groups, width):
    count, rows, _ = parts.shape
    return pl.pallas_call(
        functools.partial(join_hidden_body, groups=groups, width=width),
        out_shape=[struct((rows, groups * count * width), F32)] * 2,
        name="join_hidden",
    )(parts)


def join_captions_body(order_ref, *refs, groups, inner):
    *pieces, out_ref = refs
    width = pieces[0].shape[2]
    for at, piece in enumerate(pieces):
        for group in range(groups):
            for index in range(inner):
                column = ((group * len(pieces) + order_ref[at]) * inner + index) * width
                out_ref[:, pl.ds(pl.multiple_of(column, width), width)] = piece[group * inner + index].astype(F32)


def join_captions(pieces, order, groups, inner):
    count, rows, width = pieces[0].shape
    if width % 128:
        full = jnp.zeros((len(pieces),) + pieces[0].shape, pieces[0].dtype)
        for at, piece in enumerate(pieces):
            full = lax.dynamic_update_index_in_dim(full, piece, order[at], 0)
        full = full.reshape(len(pieces), groups, inner, rows, width).transpose(3, 1, 0, 2, 4)
        return full.reshape(rows, -1).astype(F32)
    return pl.pallas_call(
        functools.partial(join_captions_body, groups=groups, inner=inner),
        grid_spec=pltpu.PrefetchScalarGridSpec(
            num_scalar_prefetch=1,
            grid=(1,),
            in_specs=[full_spec(piece.shape) for piece in pieces],
            out_specs=full_spec((rows, len(pieces) * count * width)),
        ),
        out_shape=struct((rows, len(pieces) * count * width), F32),
        name="join_captions",
    )(order, *pieces)


def place_body(index_ref, *refs):
    *pieces, out_ref, sems = refs
    copies = [
        pltpu.make_async_copy(piece, out_ref.at[:, index_ref[at]], sems.at[at])
        for at, piece in enumerate(pieces)
    ]
    for copy in copies:
        copy.start()
    for copy in copies:
        copy.wait()


def place(pieces, order):
    groups, rows, columns = pieces[0].shape
    anywhere = pl.BlockSpec(memory_space=pl.ANY)
    return pl.pallas_call(
        place_body,
        grid_spec=pltpu.PrefetchScalarGridSpec(
            num_scalar_prefetch=1,
            grid=(),
            in_specs=[anywhere] * len(pieces),
            out_specs=anywhere,
            scratch_shapes=[pltpu.SemaphoreType.DMA((len(pieces),))],
        ),
        out_shape=struct((groups, len(pieces), rows, columns), pieces[0].dtype),
        name="place",
    )(order, *pieces)


def axes_size(axes):
    return math.prod(lax.axis_size(axis) for axis in axes)


def swap(x, axes, mask):
    return lax.ppermute(x, axes, [(i, i ^ mask) for i in range(axes_size(axes))])


def pick(x, index, axis=0):
    return lax.dynamic_index_in_dim(x, index, axis, keepdims=False)


def spread(x, axes, masks):
    first, second, fast = masks[1], masks[2], masks[4]
    half = x.shape[0] // 2
    one = swap(x, axes, first)
    two = swap(x, axes, second)
    far = jnp.concatenate([swap(two[:half], axes, first), swap(one[half:], axes, second)], axis=0)
    near = [x, one, two, far]
    return near + [swap(piece, axes, fast) for piece in near]


def collect(keep, send, axes, masks):
    first, second, fast = masks[1], masks[2], masks[4]
    half = keep.shape[2] // 2
    total = keep + swap(send, axes, fast).astype(F32)
    left, right = total[:, :, :half], total[:, :, half:]
    left_got = swap(left[1::2].astype(BF16), axes, first).astype(F32)
    right_got = swap(right[2:].astype(BF16), axes, second).astype(F32)
    left_end = swap((left[2] + left_got[1]).astype(BF16), axes, second).astype(F32)
    right_end = swap((right[1] + right_got[1]).astype(BF16), axes, first).astype(F32)
    return jnp.concatenate(
        [left[0] + left_got[0] + left_end, right[0] + right_got[0] + right_end], axis=1
    )


def collect_rows(left, right, right_dim, axes, masks):
    rows = left.shape[0] // len(masks)
    shape = (len(masks) // 2, rows, right.shape[1 - right_dim])
    middle = left.shape[0] // 2
    send = dot(left[middle:], right, 1, right_dim).astype(BF16).reshape(shape)
    keep = dot(left[:middle], right, 1, right_dim).reshape(shape)
    return collect(keep, send, axes, masks)


def turn_sum(parts, axes):
    return jnp.sum(turn(parts.astype(BF16), axes).astype(F32), axis=0)


def small_sum(x, axes):
    count = axes_size(axes)
    if count > 8 or count & (count - 1):
        return lax.psum(x, axes)
    total = x
    for mask in range(1, count):
        total = total + swap(x, axes, mask)
    return total


def clip_rows(x, axes):
    count = axes_size(axes)
    if count > 8 or count & (count - 1):
        return lax.psum_scatter(x, axes, scatter_dimension=0, tiled=False)
    me = lax.axis_index(axes)
    total = pick(x, me).astype(F32)
    for mask in range(1, count):
        total = total + swap(pick(x, me ^ mask), axes, mask).astype(F32)
    return total


def clip_spread(x, axes):
    return [swap(x, axes, mask) if mask else x for mask in range(axes_size(axes))]


def turn(x, axes):
    return lax.all_to_all(x, axes, split_axis=0, concat_axis=0, tiled=False)


def on_device(
    tokens,
    positions,
    captions,
    caption_lengths,
    conditioning,
    modulation_weight,
    modulation_bias,
    attention_gain,
    query_weight,
    key_weight,
    value_weight,
    query_gain,
    key_gain,
    text_weight,
    textkey_weight,
    textvalue_weight,
    textkey_gain,
    cross_gate,
    output_weight,
    feedforward_gain,
    gate_weight,
    up_weight,
    down_weight,
    cotangent,
):
    wide_count, narrow_count = lax.axis_size(W), lax.axis_size(N)
    clip_count = lax.axis_size(C)
    clip_index, wide_index = lax.axis_index(C), lax.axis_index(W)
    own_rows, model_width = tokens.shape[1], tokens.shape[2]
    head_size = query_gain.shape[0]
    head_count = model_width // head_size
    score_scale = head_size ** (-0.5)
    score_shift = 3.0 * math.sqrt(head_size)
    split_tokens = head_count % (wide_count * narrow_count) != 0
    tp, dp = ((N,), (C, W)) if split_tokens else (PLANE, (C,))
    tp_count, dp_count = axes_size(tp), axes_size(dp)
    tp_index = lax.axis_index(tp)
    masks = [0, 1, 4, 5, 2, 3, 6, 7]
    order = (tp_index ^ jnp.array(masks, jnp.int32)).astype(jnp.int32)
    clip_order = clip_index ^ jnp.arange(clip_count, dtype=jnp.int32)
    group_rows = own_rows * tp_count
    local_heads = head_count // tp_count
    head_width = local_heads * head_size
    weight_rows = query_weight.shape[0]
    hidden_rows, hidden_width = down_weight.shape[0], gate_weight.shape[1]
    local_hidden = hidden_width // tp_count

    def after(value, *others):
        return lax.optimization_barrier((value,) + others)[0]

    def head_columns(weight):
        return weight.reshape(weight_rows, tp_count, head_width).transpose(1, 0, 2)

    def hidden_columns(weight):
        split = weight.reshape(weight_rows, dp_count, tp_count, hidden_rows)
        return split.transpose(2, 0, 1, 3).reshape(tp_count, weight_rows, local_hidden)

    def gather_rows(rows):
        return lax.all_gather(rows, dp, axis=0, tiled=True)

    qkv_parts = turn(
        jnp.concatenate([head_columns(w) for w in (query_weight, key_weight, value_weight)], axis=2), tp
    )
    qkv_slice = gather_rows(qkv_parts.reshape(tp_count * weight_rows, 3 * head_width))

    cond_float = conditioning.astype(F32)
    cond_act = jax.nn.silu(cond_float)
    weight_float = modulation_weight.astype(F32)
    partial_mod = jnp.dot(cond_act, weight_float, precision=HIGHEST, preferred_element_type=F32)
    own_mod = small_sum(clip_rows(partial_mod, (C,)), PLANE) + modulation_bias
    shift_attn, scale_attn, gate_attn, shift_feed, scale_feed, gate_feed = jnp.split(own_mod, 6)

    place_rows = jnp.stack([positions[0] // 64, positions[0] % 64]).astype(BF16)
    place_rows = jnp.pad(place_rows, ((0, 30), (0, model_width - own_rows)))
    bundle = jnp.stack(spread(jnp.concatenate([tokens[0], cotangent[0], place_rows], axis=0), tp, masks))
    token_all = bundle[:, :own_rows].reshape(group_rows, model_width)
    cotangent_all = bundle[:, own_rows : 2 * own_rows].reshape(group_rows, model_width)
    place_all = bundle[:, 2 * own_rows : 2 * own_rows + 2, :own_rows].astype(F32)
    position_all = (place_all[:, 0] * 64.0 + place_all[:, 1]).reshape(group_rows)

    token_float = tokens[0].astype(F32)
    inv_attn = inverse_rms(token_float)
    hat_attn = token_float * inv_attn
    normed_attn = hat_attn * attention_gain
    group_float = token_all.astype(F32)
    group_normed = group_float * inverse_rms(group_float) * attention_gain
    mod_in = (group_normed * (1.0 + scale_attn) + shift_attn).astype(BF16)

    text_weights = jnp.concatenate([head_columns(w) for w in (textkey_weight, textvalue_weight)], axis=2)
    text_parts = turn(after(text_weights, qkv_parts), tp).reshape(tp_count * weight_rows, 2 * head_width)
    pieces = model_width // (2 * head_width)
    mixed_rows = jnp.concatenate(
        [text_parts, output_weight.reshape(weight_rows * pieces, 2 * head_width)], axis=0
    )
    mixed_all = gather_rows(mixed_rows).reshape(dp_count, mixed_rows.shape[0], 2 * head_width)
    text_slice = mixed_all[:, : tp_count * weight_rows].reshape(model_width, 2 * head_width)
    output_rows = mixed_all[:, tp_count * weight_rows :].reshape(dp_count * weight_rows, model_width)
    output_pieces = [
        piece.reshape(dp_count, weight_rows, model_width) for piece in spread(output_rows, tp, masks)
    ]
    output_full = place(output_pieces, order).reshape(model_width, model_width)
    hidden_weights = jnp.concatenate([hidden_columns(gate_weight), hidden_columns(up_weight)], axis=2)
    hidden_parts = turn(after(hidden_weights, text_parts), tp)
    hidden_slice = gather_rows(hidden_parts.reshape(tp_count * weight_rows, 2 * local_hidden))
    down_slice = gather_rows(after(down_weight, hidden_parts))

    caption_rows, text_width = captions.shape[1], captions.shape[2]
    text_rows = text_weight.shape[0]
    slot_count = caption_rows * narrow_count
    slot_part = slot_count // tp_count
    own_columns = pick(
        captions[0].reshape(caption_rows, clip_count, wide_count, narrow_count, text_rows), wide_index, 2
    )
    caption_parts = own_columns.transpose(1, 2, 0, 3).reshape(-1, caption_rows, text_rows)
    caption_columns = (
        turn(after(caption_parts, text_parts), (C, N))
        .reshape(clip_count, tp_count, slot_part, text_rows)
        .transpose(1, 0, 2, 3)
        .reshape(clip_count * slot_count, text_rows)
    )
    text_group = turn_sum(
        dot(caption_columns, text_weight).reshape(tp_count, clip_count * slot_part, model_width), tp
    )
    if split_tokens:
        text_group = lax.psum(text_group, W)
    text_own = clip_rows(text_group.astype(BF16).reshape(clip_count, slot_part, model_width), (C,))
    text_proj = jnp.concatenate(spread(text_own.astype(BF16), tp, masks), axis=0)
    true_slot = (order[:, None] * slot_part + jnp.arange(slot_part)).reshape(slot_count)
    keep = (true_slot < caption_lengths[clip_index]).astype(F32)

    cosine, sine = rope_tables(position_all, head_size)
    qkv_raw = dot(mod_in, qkv_slice)
    query_rot, key_rot, value_own = prepare(qkv_raw, cosine, sine, query_gain, key_gain, head_width)
    if split_tokens:
        keys_all = lax.all_gather(key_rot, W, axis=0, tiled=True)
        values_all = lax.all_gather(value_own, W, axis=0, tiled=True)
    else:
        keys_all, values_all = key_rot, value_own
    text_raw = dot(text_proj, text_slice)
    text_key, text_value = prepare_text(text_raw, textkey_gain, head_width)
    text_gate = pick(jnp.tanh(cross_gate).reshape(tp_count, local_heads), tp_index)
    gate_lanes = jnp.repeat(text_gate, head_size)
    mixed, own_out, cross_out, denom, text_denom = attend(
        order, query_rot, keys_all, values_all, text_key, text_value, keep, gate_lanes, head_size
    )

    mixed_own = turn(mixed, tp).transpose(1, 0, 2).reshape(own_rows, model_width)
    attn_out = dot(mixed_own, output_full)
    resid = token_float + gate_attn * attn_out
    inv_feed = inverse_rms(resid)
    hat_feed = resid * inv_feed
    normed_feed = hat_feed * feedforward_gain
    mod_own = (normed_feed * (1.0 + scale_feed) + shift_feed).astype(BF16)
    mod_ff = jnp.concatenate(spread(mod_own, tp, masks), axis=0)

    hidden_pre = dot(mod_ff, hidden_slice)
    gate_pre, up_pre = hidden_pre[:, :local_hidden], hidden_pre[:, local_hidden:]
    sigmoid_gate = jax.nn.sigmoid(gate_pre)
    silu_gate = gate_pre * sigmoid_gate
    inner = (silu_gate * up_pre).astype(BF16)
    dfeed = (gate_feed * cotangent_all.astype(F32)).astype(BF16)
    dinner = dot(dfeed, down_slice, 1, 1)
    dgate_pre = (dinner * up_pre * (sigmoid_gate * (1.0 + gate_pre * (1.0 - sigmoid_gate)))).astype(BF16)
    dup_pre = (dinner * silu_gate).astype(BF16)
    dhidden = jnp.concatenate([dgate_pre, dup_pre], axis=1)
    dmod_ff = collect_rows(dhidden, hidden_slice, 1, tp, masks)

    def scatter_rows(grads):
        return lax.psum_scatter(grads.astype(BF16), dp, scatter_dimension=0, tiled=True)

    dhidden_rows = scatter_rows(dot(mod_ff, dhidden, 0, 0))
    downweight_grad = scatter_rows(dot(inner, dfeed, 0, 0)).astype(F32)

    dout = cotangent[0].astype(F32)
    dshift_feed = jnp.sum(dmod_ff, axis=0)
    dscale_feed = jnp.sum(dmod_ff * normed_feed, axis=0)
    dfeed_gain, dresid_norm = norm_backward(
        hat_feed, inv_feed, feedforward_gain, dmod_ff * (1.0 + scale_feed)
    )
    dresid = dout + dresid_norm
    dgate_attn = jnp.sum(dresid * attn_out, axis=0)
    dattn = (gate_attn * dresid).astype(BF16)

    dmixed_own = dot(dattn, output_full, 1, 1).astype(BF16)
    dmixed = turn(dmixed_own.reshape(own_rows, tp_count, head_width).transpose(1, 0, 2), tp)
    dquery_text, dtext_key, dtext_value, dgate_lanes = attend_back(
        order, query_rot, cross_out, text_denom, dmixed, text_key, text_value, head_size, text=(keep, gate_lanes)
    )
    dquery, dkey, dvalue = attend_back(
        order, query_rot, own_out, denom, dmixed, keys_all, values_all, head_size, start=dquery_text
    )
    if split_tokens:
        dkey = lax.psum_scatter(dkey.astype(BF16), W, scatter_dimension=0, tiled=True)
        dvalue = lax.psum_scatter(dvalue.astype(BF16), W, scatter_dimension=0, tiled=True)
        dtext_key, dtext_value = lax.psum((dtext_key, dtext_value), W)
    dcross_gate = jnp.sum(dgate_lanes.reshape(local_heads, head_size), axis=1) * (1.0 - text_gate * text_gate)
    dqkv, gain_grads = finish(qkv_raw, dquery, dkey, dvalue, cosine, sine, query_gain, key_gain)
    dmod_in = collect_rows(dqkv, qkv_slice, 1, tp, masks)

    dtext_heads, dtkey_gain = finish_text(text_raw, dtext_key, dtext_value, textkey_gain)
    dtext_parts = dot(dtext_heads, text_slice, 1, 1).reshape(tp_count, slot_part, model_width)
    dtext_own = jnp.zeros_like(dtext_parts)
    for at in range(tp_count):
        dtext_own = lax.dynamic_update_index_in_dim(dtext_own, dtext_parts[at], order[at], 0)
    dtext_group = turn_sum(dtext_own, tp).astype(BF16)
    dtext_clips = clip_spread(dtext_group, (C,))
    dtext_rows = jnp.zeros((clip_count, slot_part, model_width), BF16)
    for at in range(clip_count):
        dtext_rows = lax.dynamic_update_index_in_dim(dtext_rows, dtext_clips[at], clip_order[at], 0)
    dtext_pieces = spread(dtext_rows.reshape(clip_count * slot_part, model_width), tp, masks)
    dtext_all = place([piece[None] for piece in dtext_pieces], order).reshape(-1, model_width)
    textweight_grad = dot(caption_columns, dtext_all, 0, 0)
    dcaption_parts = (
        dot(dtext_all, text_weight, 1, 1)
        .astype(BF16)
        .reshape(tp_count, clip_count, slot_part, text_rows)
        .transpose(1, 0, 2, 3)
        .reshape(-1, caption_rows, text_rows)
    )
    dcaption_own = turn(dcaption_parts, (C, N))
    wide_order = (wide_index ^ jnp.arange(wide_count, dtype=jnp.int32)).astype(jnp.int32)
    captions_grad = join_captions(clip_spread(dcaption_own, (W,)), wide_order, clip_count, narrow_count)

    feed_out = collect_rows(after(inner, dmod_ff), down_slice, 0, tp, masks)
    block_output = resid + gate_feed * feed_out
    dgate_feed = jnp.sum(dout * feed_out, axis=0)

    dout_parts = (
        dot(after(mixed_own, dmixed), dattn, 0, 0)
        .astype(BF16)
        .reshape(dp_count, tp_count, weight_rows, model_width)
        .transpose(1, 0, 2, 3)
        .reshape(tp_count, dp_count * weight_rows, model_width)
    )
    dout_group = turn_sum(dout_parts, tp)
    outweight_grad = clip_rows(
        dout_group.astype(BF16).reshape(dp_count, weight_rows, model_width), dp
    ).astype(F32)
    shared = 1.0 / wide_count if split_tokens else 1.0
    dhead_rows = scatter_rows(
        jnp.concatenate([dot(mod_in, dqkv, 0, 0), dot(text_proj, dtext_heads, 0, 0) * shared], axis=1)
    )
    dhidden_parts = turn(dhidden_rows.reshape(tp_count, weight_rows, 2 * local_hidden), tp)
    gateweight_grad, upweight_grad = join_hidden(dhidden_parts, dp_count, hidden_rows)
    dhead_parts = turn(dhead_rows.reshape(tp_count, weight_rows, 5 * head_width), tp)
    queryweight_grad, keyweight_grad, valueweight_grad, textkey_grad, textvalue_grad = join_heads(
        dhead_parts, head_width
    )

    dshift_attn = jnp.sum(dmod_in, axis=0)
    dscale_attn = jnp.sum(dmod_in * normed_attn, axis=0)
    dattn_gain, dtokens_norm = norm_backward(
        hat_attn, inv_attn, attention_gain, dmod_in * (1.0 + scale_attn)
    )
    tokens_grad = dresid + dtokens_norm

    head_range = jnp.arange(head_count) - tp_index * local_heads
    dgate_rows = jnp.sum(
        jnp.where(head_range[:, None] == jnp.arange(local_heads)[None, :], dcross_gate[None, :], 0.0), axis=1
    )
    pad = -head_count % head_size
    small = jnp.concatenate(
        [
            dshift_attn,
            dscale_attn,
            dgate_attn,
            dshift_feed,
            dscale_feed,
            dgate_feed,
            dattn_gain,
            dfeed_gain,
            gain_grads[0],
            gain_grads[1],
            dtkey_gain[0] * shared,
            dgate_rows,
            jnp.zeros((pad,), F32),
        ]
    )
    clip_small = jnp.stack(clip_spread(small_sum(small, PLANE), (C,)))
    mod_width = 6 * model_width
    dmod_all = clip_small[:, :mod_width]
    gains = jnp.sum(clip_small[:, mod_width:], axis=0)
    attngain_grad, feedgain_grad = gains[:model_width], gains[model_width : 2 * model_width]
    rest = gains[2 * model_width :]
    querygain_grad, keygain_grad, textgain_grad = (
        rest[:head_size],
        rest[head_size : 2 * head_size],
        rest[2 * head_size : 3 * head_size],
    )
    crossgate_grad = rest[3 * head_size : 3 * head_size + head_count]
    cond_rows = jnp.stack([pick(cond_act, clip_order[at]) for at in range(clip_count)])
    modweight_grad = jnp.dot(cond_rows.T, dmod_all, precision=HIGHEST, preferred_element_type=F32)
    dcond_rows = jnp.dot(dmod_all, weight_float.T, precision=HIGHEST, preferred_element_type=F32)
    dcond_act = jnp.stack([pick(dcond_rows, clip_order[at]) for at in range(clip_count)])
    sigmoid_cond = jax.nn.sigmoid(cond_float)
    conditioning_grad = dcond_act * sigmoid_cond * (1.0 + cond_float * (1.0 - sigmoid_cond))
    modbias_grad = jnp.sum(dmod_all, axis=0)
    return (
        block_output[None],
        tokens_grad[None],
        captions_grad[None],
        conditioning_grad,
        modweight_grad,
        modbias_grad,
        attngain_grad,
        queryweight_grad,
        keyweight_grad,
        valueweight_grad,
        querygain_grad,
        keygain_grad,
        textweight_grad,
        textkey_grad,
        textvalue_grad,
        textgain_grad,
        crossgate_grad,
        outweight_grad,
        feedgain_grad,
        gateweight_grad,
        upweight_grad,
        downweight_grad,
    )


def solution(mesh):
    rows, whole = P(ALL, None), P()
    tokens, captions = P(C, PLANE, None), P(C, N, None)
    columns = P(None, ALL)
    return jax.shard_map(
        on_device,
        mesh=mesh,
        in_specs=(
            tokens,
            P(C, PLANE),
            captions,
            whole,
            columns,
            rows,
            whole,
            whole,
            rows,
            rows,
            rows,
            whole,
            whole,
            rows,
            rows,
            rows,
            whole,
            whole,
            rows,
            whole,
            rows,
            rows,
            rows,
            tokens,
        ),
        out_specs=(
            tokens,
            tokens,
            captions,
            columns,
            rows,
            whole,
            whole,
            rows,
            rows,
            rows,
            whole,
            whole,
            rows,
            rows,
            rows,
            whole,
            whole,
            rows,
            whole,
            rows,
            rows,
            rows,
        ),
        check_vma=False,
    )
```

time: 672 us -> 867 us (1.29)
  Pallas kernels: 0 us -> 304 us
  local copies, waits for them, and re-layouts: 190 us -> 85.8 us
  blocking collectives: 27.2 us -> 0 us
  between operations: 17.3 us -> 38.5 us
  waiting for transfers between devices: 131 us -> 147 us
  starting transfers between devices: 149 us -> 137 us
  matrix products: 88.9 us -> 79.3 us
    pallas_call x0 -> x12, Pallas kernels: none -> 304 us  [the longest x2 242 us: place(): pl.pallas_call(place_body, grid_spec=pltpu.PrefetchScalarGridSpec(num_sca...]
    dynamic_update_slice x62 -> x12, local copies, waits for them, and re-layouts: 42.3 us -> 5.22 us  [the longest x8 5.17 us: on_device(): lax.dynamic_update_index_in_dim(dtext_own, dtext_parts[at], order[at], 0)]
    ppermute x144 -> x87, starting transfers between devices: 120 us -> 85.7 us  [swap(): lax.ppermute(x, axes, [(i, i ^ mask) for i in range(axes_size(axes))])]
    all_to_all x2 -> x0, blocking collectives: 27.2 us -> none  [turn(): return lax.all_to_all(x, axes, split_axis=0, concat_axis=0, tiled=False)]
    dot_general x13 -> x1, matrix products: 27.2 us -> 2.18 us  [on_device(): jnp.dot(cond_rows.T, dmod_all, precision=HIGHEST, preferred_element_type=...]
    all_to_all x7 -> x12, starting transfers between devices: 27 us -> 49.7 us  [turn(): return lax.all_to_all(x, axes, split_axis=0, concat_axis=0, tiled=False)]
    convert_element_type x15 -> x2, local copies, waits for them, and re-layouts: 19.6 us -> 1.43 us  [on_device(): keep = (true_slot < caption_lengths[clip_index]).astype(F32)]
    dot_general x18 -> x21, matrix products: 60.2 us -> 75.6 us  [dot(): lax.dot_general(left, right, (((left_dim,), (right_dim,)), ((), ())), pre...]
  transfers between devices with their start and end apart: 159 -> 106, of which waited for: 44 -> 36; matrix products, arithmetic and copies ran while one was open for 42% -> 25% of each run, Pallas kernels for 0% -> 35%
where the time goes in v1:
time: 867 us; the launch traced here: 858 us
  Pallas kernels  304 us (35%)
  waiting for transfers between devices  147 us (17%)
  starting transfers between devices  137 us (16%)
  local copies, waits for them, and re-layouts  85.8 us (10%)
  matrix products  79.3 us (9%)
  other arithmetic  66.5 us (8%)
  between operations  38.5 us (4%)
    pallas_call x2, Pallas kernels, place(): pl.pallas_call(place_body, grid_spec=pltpu.PrefetchScalarGridSpec(num_sca...  242 us
    ppermute x87, waiting for transfers between devices, swap(): lax.ppermute(x, axes, [(i, i ^ mask) for i in range(axes_size(axes))])  114 us
    ppermute x87, starting transfers between devices, swap(): lax.ppermute(x, axes, [(i, i ^ mask) for i in range(axes_size(axes))])  85.7 us
    dot_general x21, matrix products, dot(): lax.dot_general(left, right, (((left_dim,), (right_dim,)), ((), ())), pre...  75.6 us
    all_to_all x12, starting transfers between devices, turn(): return lax.all_to_all(x, axes, split_axis=0, concat_axis=0, tiled=False)  49.7 us
    all_to_all x12, waiting for transfers between devices, turn(): return lax.all_to_all(x, axes, split_axis=0, concat_axis=0, tiled=False)  32.1 us
    unnamed x172, local copies, waits for them, and re-layouts  31.3 us
    pallas_call x2, Pallas kernels, attend_back(): pl.pallas_call(body, grid_spec=pltpu.PrefetchScalarGridSpec(num_scalar_pr...  21.5 us
  transfers between devices with their start and end apart: 106, of which 36 were waited for; matrix products, arithmetic and copies ran while one was open for 25% of the time, Pallas kernels for 35%

profile of v1, /device:TPU:0, one launch (start us, length us, event | category | flops | bytes accessed | tf_op | source)
XLA Modules:
  0.0 857.8 jit_solution(13190132832176368776)
XLA Ops:
  11.8 5.3 all-to-all-start
  17.7 8.3 all-to-all-done
  73.2 5.2 all-to-all-start.2
  119.9 5.6 fusion.108
  130.2 16.5 %all-to-all-done.3 = bf16[8,128,1536]{2,1,0:T(8,128)(2,1)} async-done(((bf16[8,128,1536]{2,1,0:T(8,128)(2,1)}), bf16[8,128,1536]{2,1,0:T(8,128)(2,1)}, u32[]{:S(2)}, u32[]{:S(2)}) %all-to-all-start.3) | async-done | bytes 3145760 | tf_op jit(solution)/shard_map/all_to_all | solution.py:512
  161.8 6.1 collective-permute-done.19
  169.5 6.7 fusion.114.raw_ref
  176.2 8.3 prepare.1
  192.3 5.2 collective-permute-done.23
  212.2 8.7 %attend.1 = (bf16[8,128,192]{2,1,0:T(8,128)(2,1)}, f32[1024,192]{1,0:T(8,128)}, f32[1024,192]{1,0:T(8,128)}, f32[1024,192]{1,0:T(8,128)}, f32[1024,192]{1,0:T(8,128)}) custom-call(s32[8]{0:T(128)} %copy-done.42, bf16[1024,192]{1,0:T(8,128)(2,1)} %get-tuple-element.56.query_ref, bf16[1024,192]{1,0:T(8,128)(2,1)} %get-tuple-element.57.key_ref, ...), custom_call_target="tpu_custom_call" | custom-call | tf_op jit(solution)/shard_map/attend/pallas_call | solution.py:169
  253.7 144.9 %place.2 = bf16[4,8,48,1536]{3,2,1,0:T(8,128)(2,1)} custom-call(s32[8]{0:T(128)} %copy-done.42, bf16[4,48,1536]{2,1,0:T(8,128)(2,1)} %reshape_reshape.3.refs_0_, bf16[4,48,1536]{2,1,0:T(8,128)(2,1)} %bitcast.45.refs_1_, bf16[4,48,1536]{2,1,0:T(8,128)(2,1)} %bitcast.46.refs_2_, bf16[4,48,1536]{2,1,0:T(8,128)(2,1)} %bitcast.47.refs_3_, ...), custom_call_target="tpu_custom_call" | custom-call | tf_op jit(solution)/shard_map/place/pallas_call | solution.py:423
  409.9 5.6 collective-permute-done.38
  427.7 8.4 fusion.116
  436.1 6.2 multiply_convert_fusion
  465.4 5.1 collective-permute-done.46
  495.9 7.6 convolution_convert_fusion.2
  504.6 7.8 text_back.1
  526.9 13.7 %attend_back.1 = (f32[1024,192]{1,0:T(8,128)}, f32[1024,192]{1,0:T(8,128)}, f32[1024,192]{1,0:T(8,128)}) custom-call(s32[8]{0:T(128)} %copy-done.42, bf16[1024,192]{1,0:T(8,128)(2,1)} %get-tuple-element.56.query_ref, f32[1024,192]{1,0:T(8,128)} %get-tuple-element.67.out_ref, f32[1024,192]{1,0:T(8,128)} %get-tuple-element.68.denom_ref, ...), custom_call_target="tpu_custom_call" | custom-call | tf_op jit(solution)/shard_map/attend_back/pallas_call | solution.py:256
  540.6 11.2 %finish.1 = (bf16[1024,576]{1,0:T(8,128)(2,1)}, f32[2,64]{1,0:T(2,128)}) custom-call(f32[1024,576]{1,0:T(8,128)} %fusion.114.raw_ref, f32[1024,192]{1,0:T(8,128)} %get-tuple-element.72.dquery_ref, f32[1024,192]{1,0:T(8,128)} %get-tuple-element.73.dkey_ref, f32[1024,192]{1,0:T(8,128)} %get-tuple-element.74.dvalue_ref, f32[1024,64]{1,0:T(8,128)} %get-tuple-element.189.cos_ref, ...), custom_call_target="tpu_custom_call" | custom-call | tf_op jit(solution)/shard_map/finish/pallas_call | solution.py:314
  564.1 7.0 collective-permute-start.60
  574.3 7.4 collective-permute-done.61
  601.9 5.0 collective-permute-done.63
  621.9 97.3 %place.3 = bf16[1,8,128,1536]{3,2,1,0:T(8,128)(2,1)} custom-call(s32[8]{0:T(128)} %copy-done.42, bf16[1,128,1536]{2,1,0:T(8,128)(2,1)} %bitcast.328, bf16[1,128,1536]{2,1,0:T(8,128)(2,1)} %bitcast.334, bf16[1,128,1536]{2,1,0:T(8,128)(2,1)} %bitcast.333, bf16[1,128,1536]{2,1,0:T(8,128)(2,1)} %bitcast.335, bf16[1,128,1536]{2,1,0:T(8,128)(2,1)} %bitcast.341, ...), custom_call_target="tpu_custom_call" | custom-call | tf_op jit(solution)/shard_map/place/pallas_call | solution.py:423
  755.5 42.9 %collective-permute-done.74 = f32[12544]{0:T(1024)S(1)} collective-permute-done((f32[12544]{0:T(1024)S(1)}, f32[12544]{0:T(1024)S(1)}, u32[]{:S(2)}, u32[]{:S(2)}) %collective-permute-start.74) | collective-permute-done | bytes 50208 | tf_op jit(solution)/shard_map/ppermute | solution.py:442
  (564 shorter events, 373.5 us)
Async XLA Ops:
  30.3 125.3 %all-gather.7.cloned.1.call-start = ((), (), s32[]{:S(2)}) async-start(), calls=%async_computation.16 | async-start | bytes 2211840 | tf_op jit(solution)/shard_map/all_gather | solution.py:574
  31.3 49.9 %collective-permute-start.10 = (bf16[288,1536]{1,0:T(8,128)(2,1)}, bf16[288,1536]{1,0:T(8,128)(2,1)S(1)}, u32[]{:S(2)}, u32[]{:S(2)}) collective-permute-start(bf16[288,1536]{1,0:T(8,128)(2,1)} %pad_maximum_fusion.3), channel_id=1, source_target_pairs={{0,1},{1,0},{2,3},{3,2},{4,5},{5,4},{6,7},{7,6},{8,9},{9,8},{10,11... | collective-permute-start | bytes 2654216 | tf_op jit(solution)/shard_map/ppermute | solution.py:442
  33.2 45.2 %collective-permute-start.11 = (bf16[288,1536]{1,0:T(8,128)(2,1)}, bf16[288,1536]{1,0:T(8,128)(2,1)S(1)}, u32[]{:S(2)}, u32[]{:S(2)}) collective-permute-start(bf16[288,1536]{1,0:T(8,128)(2,1)} %pad_maximum_fusion.3), channel_id=1, source_target_pairs={{0,4},{1,5},{2,6},{3,7},{4,0},{5,1},{6,2},{7,3},{8,12},{9,13},{10,... | collective-permute-start | bytes 2654216 | tf_op jit(solution)/shard_map/ppermute | solution.py:442
  39.1 130.4 %all-gather.5.cloned.1.call-start = ((), (), s32[]{:S(2)}) async-start(), calls=%async_computation.15 | async-start | bytes 2457600 | tf_op jit(solution)/shard_map/all_gather | solution.py:574
  104.8 41.9 %all-to-all-start.3 = ((bf16[8,128,1536]{2,1,0:T(8,128)(2,1)}), bf16[8,128,1536]{2,1,0:T(8,128)(2,1)}, u32[]{:S(2)}, u32[]{:S(2)}) async-start(bf16[8,128,1536]{2,1,0:T(8,128)(2,1)} %convolution_convert_fusion.1), calls=%async_computation.3 | async-start | bytes 6291456 | tf_op jit(solution)/shard_map/all_to_all | solution.py:512
  109.3 318.5 %all-gather.9.cloned.1.call-start = ((), (), s32[]{:S(2)}) async-start(), calls=%async_computation.17 | async-start | bytes 3932160 | tf_op jit(solution)/shard_map/all_gather | solution.py:574
  186.0 67.7 %collective-permute-start.33 = (bf16[192,1536]{1,0:T(8,128)(2,1)}, bf16[192,1536]{1,0:T(8,128)(2,1)}, u32[]{:S(2)}, u32[]{:S(2)}) collective-permute-start(bf16[192,1536]{1,0:T(8,128)(2,1)} %reshape.373), channel_id=1, source_target_pairs={{0,2},{1,3},{2,0},{3,1},{4,6},{5,7},{6,4},{7,5},{8,10},{9,11},{10,... | collective-permute-start | bytes 1769480 | tf_op jit(solution)/shard_map/ppermute | solution.py:442
  191.4 62.3 %collective-permute-start.34 = (bf16[192,1536]{1,0:T(8,128)(2,1)}, bf16[192,1536]{1,0:T(8,128)(2,1)}, u32[]{:S(2)}, u32[]{:S(2)}) collective-permute-start(bf16[192,1536]{1,0:T(8,128)(2,1)} %collective-permute-done.29), channel_id=1, source_target_pairs={{0,2},{1,3},{2,0},{3,1},{4,6},{5,7},{6,4},{7,5},{8,10},{9,11},{10,... | collective-permute-start | bytes 1769480 | tf_op jit(solution)/shard_map/ppermute | solution.py:442
  205.8 47.9 %collective-permute-start.35 = (bf16[192,1536]{1,0:T(8,128)(2,1)}, bf16[192,1536]{1,0:T(8,128)(2,1)}, u32[]{:S(2)}, u32[]{:S(2)}) collective-permute-start(bf16[192,1536]{1,0:T(8,128)(2,1)} %collective-permute-done.30), channel_id=1, source_target_pairs={{0,2},{1,3},{2,0},{3,1},{4,6},{5,7},{6,4},{7,5},{8,10},{9,11},{10,... | collective-permute-start | bytes 1769480 | tf_op jit(solution)/shard_map/ppermute | solution.py:442
  207.8 45.9 %collective-permute-start.36 = (bf16[192,1536]{1,0:T(8,128)(2,1)}, bf16[192,1536]{1,0:T(8,128)(2,1)}, u32[]{:S(2)}, u32[]{:S(2)}) collective-permute-start(bf16[192,1536]{1,0:T(8,128)(2,1)} %constant_dynamic-update-slice_fusion.11), channel_id=1, source_target_pairs={{0,2},{1,3},{2,0},{3,1},{4,6},{5,7},{6,4},{7,5},{8,10},{9,11},{10,... | collective-permute-start | bytes 1769480 | tf_op jit(solution)/shard_map/ppermute | solution.py:442
  222.9 175.8 %all-to-all-start.4 = ((bf16[8,128,192]{1,2,0:T(8,128)(2,1)}), bf16[8,128,192]{1,2,0:T(8,128)(2,1)S(1)}, u32[]{:S(2)}, u32[]{:S(2)}) async-start(bf16[8,128,192]{1,2,0:T(8,128)(2,1)} %copy.131), calls=%async_computation.4 | async-start | bytes 786432 | tf_op jit(solution)/shard_map/all_to_all | solution.py:512
  226.8 209.3 %all-gather.11.cloned.1.call-start = ((), (), s32[]{:S(2)}) async-start(), calls=%async_computation.18 | async-start | bytes 1966080 | tf_op jit(solution)/shard_map/all_gather | solution.py:574
  252.0 483.8 %reduce-scatter.8.cloned.1.call-start = ((), (), s32[]{:S(2)}) async-start(), calls=%async_computation.20 | async-start | bytes 1966080 | tf_op jit(solution)/shard_map/reduce_scatter | solution.py:684
  495.8 319.2 %reduce-scatter.6.cloned.1.call-start = ((), (), s32[]{:S(2)}) async-start(), calls=%async_computation.19 | async-start | bytes 3932160 | tf_op jit(solution)/shard_map/reduce_scatter | solution.py:684
  526.6 305.1 %reduce-scatter.10.cloned.1.call-start = ((), (), s32[]{:S(2)}) async-start(), calls=%async_computation.21 | async-start | bytes 3932160 | tf_op jit(solution)/shard_map/reduce_scatter | solution.py:684
  556.2 56.6 %collective-permute-start.55 = (bf16[4,128,1536]{2,1,0:T(8,128)(2,1)}, bf16[4,128,1536]{2,1,0:T(8,128)(2,1)}, u32[]{:S(2)}, u32[]{:S(2)}) collective-permute-start(bf16[4,128,1536]{2,1,0:T(8,128)(2,1)} %bitcast.73), channel_id=1, source_target_pairs={{0,2},{1,3},{2,0},{3,1},{4,6},{5,7},{6,4},{7,5},{8,10},{9,11},{10,... | collective-permute-start | bytes 4718600 | tf_op jit(solution)/shard_map/ppermute | solution.py:442
  618.3 109.3 %collective-permute-start.56 = (bf16[2,128,768]{2,1,0:T(8,128)(2,1)}, bf16[2,128,768]{2,1,0:T(8,128)(2,1)}, u32[]{:S(2)}, u32[]{:S(2)}) collective-permute-start(bf16[2,128,768]{2,1,0:T(8,128)(2,1)} %slice.375), channel_id=1, source_target_pairs={{0,1},{1,0},{2,3},{3,2},{4,5},{5,4},{6,7},{7,6},{8,9},{9,8},{10,11... | collective-permute-start | bytes 1179656 | tf_op jit(solution)/shard_map/ppermute | solution.py:442
  619.7 108.8 %collective-permute-start.58 = (bf16[2,128,768]{2,1,0:T(8,128)(2,1)}, bf16[2,128,768]{2,1,0:T(8,128)(2,1)}, u32[]{:S(2)}, u32[]{:S(2)}) collective-permute-start(bf16[2,128,768]{2,1,0:T(8,128)(2,1)} %slice.471), channel_id=1, source_target_pairs={{0,4},{1,5},{2,6},{3,7},{4,0},{5,1},{6,2},{7,3},{8,12},{9,13},{10,... | collective-permute-start | bytes 1179656 | tf_op jit(solution)/shard_map/ppermute | solution.py:442
  738.4 76.6 %all-to-all-start.10 = ((bf16[8,192,1536]{2,1,0:T(8,128)(2,1)}), bf16[8,192,1536]{2,1,0:T(8,128)(2,1)}, u32[]{:S(2)}, u32[]{:S(2)}) async-start(bf16[8,192,1536]{2,1,0:T(8,128)(2,1)} %bitcast.298), calls=%async_computation.10 | async-start | bytes 9437184 | tf_op jit(solution)/shard_map/all_to_all | solution.py:512
  746.5 51.8 %collective-permute-start.74 = (f32[12544]{0:T(1024)S(1)}, f32[12544]{0:T(1024)S(1)}, u32[]{:S(2)}, u32[]{:S(2)}) collective-permute-start(f32[12544]{0:T(1024)S(1)} %concatenate.81), channel_id=1, source_target_pairs={{0,1},{1,0},{2,3},{3,2},{4,5},{5,4},{6,7},{7,6},{8,9},{9,8},{10,11... | collective-permute-start | bytes 150536 | tf_op jit(solution)/shard_map/ppermute | solution.py:442
  748.4 50.2 %collective-permute-start.75 = (f32[12544]{0:T(1024)S(1)}, f32[12544]{0:T(1024)S(1)}, u32[]{:S(2)}, u32[]{:S(2)}) collective-permute-start(f32[12544]{0:T(1024)S(1)} %concatenate.81), channel_id=1, source_target_pairs={{0,2},{1,3},{2,0},{3,1},{4,6},{5,7},{6,4},{7,5},{8,10},{9,11},{10,... | collective-permute-start | bytes 150536 | tf_op jit(solution)/shard_map/ppermute | solution.py:442
  751.9 47.7 %collective-permute-start.76 = (f32[12544]{0:T(1024)S(1)}, f32[12544]{0:T(1024)S(1)}, u32[]{:S(2)}, u32[]{:S(2)}) collective-permute-start(f32[12544]{0:T(1024)S(1)} %concatenate.81), channel_id=1, source_target_pairs={{0,3},{1,2},{2,1},{3,0},{4,7},{5,6},{6,5},{7,4},{8,11},{9,10},{10,... | collective-permute-start | bytes 150536 | tf_op jit(solution)/shard_map/ppermute | solution.py:442
  752.2 47.4 %collective-permute-start.77 = (f32[12544]{0:T(1024)S(1)}, f32[12544]{0:T(1024)S(1)}, u32[]{:S(2)}, u32[]{:S(2)}) collective-permute-start(f32[12544]{0:T(1024)S(1)} %concatenate.81), channel_id=1, source_target_pairs={{0,4},{1,5},{2,6},{3,7},{4,0},{5,1},{6,2},{7,3},{8,12},{9,13},{10,... | collective-permute-start | bytes 150536 | tf_op jit(solution)/shard_map/ppermute | solution.py:442
  754.1 47.0 %collective-permute-start.78 = (f32[12544]{0:T(1024)S(1)}, f32[12544]{0:T(1024)S(1)}, u32[]{:S(2)}, u32[]{:S(2)}) collective-permute-start(f32[12544]{0:T(1024)S(1)} %concatenate.81), channel_id=1, source_target_pairs={{0,5},{1,4},{2,7},{3,6},{4,1},{5,0},{6,3},{7,2},{8,13},{9,12},{10,... | collective-permute-start | bytes 150536 | tf_op jit(solution)/shard_map/ppermute | solution.py:442
  (155 other events, 2050.8 us)
Sparse Core Ops, SparseCore 0:
  39.2 40.6 all-gather.6
  82.1 42.0 all-gather.4
  126.3 70.5 all-gather.8
  252.1 42.6 all-gather.10
  451.4 40.0 reduce-scatter.7
  503.7 65.8 reduce-scatter.5
  595.9 59.3 reduce-scatter.9

commit v2 on v1

v2 whole, which is shorter than its diff:
```python
import functools
import math

import jax
import jax.numpy as jnp
import numpy as np
from jax import lax
from jax.experimental import pallas as pl
from jax.experimental.pallas import tpu as pltpu
from jax.sharding import PartitionSpec as P

EPSILON = 1e-06
ROPE_BASE = 10000.0
C, W, N = "clip", "wide", "narrow"
ALL = (C, W, N)
PLANE = (W, N)
BF16, F32 = jnp.bfloat16, jnp.float32
HIGHEST = lax.Precision.HIGHEST


def dot(left, right, left_dim=1, right_dim=0):
    return lax.dot_general(
        left, right, (((left_dim,), (right_dim,)), ((), ())), preferred_element_type=F32
    )


def inverse_rms(values):
    return lax.rsqrt(jnp.mean(values * values, axis=-1, keepdims=True) + EPSILON)


def norm_backward(normed, inv_scale, gain, upstream):
    gain_grad = jnp.sum((upstream * normed).reshape(-1, normed.shape[-1]), axis=0)
    scaled = upstream * gain
    values_grad = inv_scale * (scaled - normed * jnp.mean(scaled * normed, axis=-1, keepdims=True))
    return (gain_grad, values_grad)


def rope_tables(positions, head_size, width):
    half_size = head_size // 2
    frequency = jnp.exp(-math.log(ROPE_BASE) * 2.0 * jnp.arange(half_size, dtype=F32) / head_size)
    angles = positions.astype(F32)[:, None] * jnp.tile(frequency, width // half_size)[None, :]
    sign = jnp.where(jnp.arange(width) % head_size < half_size, -1.0, 1.0)
    return (jnp.cos(angles), jnp.sin(angles) * sign[None, :])


def exact_dot(left, right):
    high = left.astype(BF16)
    low = (left - high.astype(F32)).astype(BF16)
    return dot(high, right) + dot(low, right)


def head_means(width, size):
    at = np.arange(width)
    return jnp.asarray((at[:, None] // size == at[None, :] // size) / size, BF16)


def half_swaps(width, size):
    at = np.arange(width)
    other = np.where(at % size < size // 2, at + size // 2, at - size // 2)
    return jnp.asarray(at[:, None] == other[None, :], BF16)


def widen(table, width):
    return jnp.concatenate([table] * (width // table.shape[1]), axis=1)


def full_spec(shape):
    return pl.BlockSpec(shape, lambda *_: (0,) * len(shape))


def row_spec(rows, width):
    return pl.BlockSpec((rows, width), lambda i, *_: (i, 0))


def struct(shape, dtype):
    return jax.ShapeDtypeStruct(shape, dtype)


def head_parts(width, size):
    return [slice(at, at + size) for at in range(0, width, size)]


def prepare_body(raw_ref, cos_ref, sin_ref, gain_ref, means_ref, swaps_ref, out_ref, value_ref):
    width = out_ref.shape[1]
    raw = raw_ref[:, :width]
    inv = lax.rsqrt(exact_dot(raw * raw, means_ref[...]) + EPSILON)
    normed = raw * inv * gain_ref[...]
    swapped = exact_dot(normed, swaps_ref[...])
    cosine, sine = widen(cos_ref[...], width), widen(sin_ref[...], width)
    out_ref[...] = (normed * cosine + swapped * sine).astype(BF16)
    value_ref[...] = raw_ref[:, width:].astype(BF16)


def prepare(raw, cosine, sine, gain, size):
    rows, width = raw.shape[0], gain.shape[0]
    block = math.gcd(rows, 256)
    return pl.pallas_call(
        prepare_body,
        grid=(rows // block,),
        in_specs=[
            row_spec(block, raw.shape[1]),
            row_spec(block, cosine.shape[1]),
            row_spec(block, cosine.shape[1]),
            full_spec((1, width)),
            full_spec((width, width)),
            full_spec((width, width)),
        ],
        out_specs=[row_spec(block, width), row_spec(block, raw.shape[1] - width)],
        out_shape=[struct((rows, width), BF16), struct((rows, raw.shape[1] - width), BF16)],
        name="prepare",
    )(raw, cosine, sine, gain[None], head_means(width, size), half_swaps(width, size))


def prepare_text_body(raw_ref, gain_ref, key_ref, value_ref):
    width, size = key_ref.shape[1], gain_ref.shape[1]
    raw, gain = raw_ref[...], gain_ref[...]
    heads = [raw[:, part] for part in head_parts(width, size)]
    heads = [head * inverse_rms(head) * gain for head in heads]
    key_ref[...] = jnp.concatenate(heads, axis=1).astype(BF16)
    value_ref[...] = raw[:, width:].astype(BF16)


def prepare_text(raw, gain, width):
    return pl.pallas_call(
        prepare_text_body, out_shape=[struct((raw.shape[0], width), BF16)] * 2, name="prepare_text"
    )(raw, gain[None])


def weights_of(left, right, factor, offset):
    scores = lax.dot_general(left, right, (((1,), (1,)), ((), ())), preferred_element_type=F32)
    return jnp.exp2(scores * factor - offset)


def attend_body(query_ref, key_ref, value_ref, out_ref, denom_ref, *, size, base, factor, offset):
    rows, width = out_ref.shape
    outs, denoms = [], []
    for part in head_parts(width, size):
        keys = key_ref[:, base + part.start : base + part.stop]
        wts = weights_of(query_ref[:, part], keys, factor, offset)
        denom = jnp.sum(wts, axis=1, keepdims=True)
        outs.append(dot(wts.astype(BF16), value_ref[:, part]) / denom)
        denoms.append(jnp.broadcast_to(denom, (rows, size)))
    out_ref[...] = jnp.concatenate(outs, axis=1)
    denom_ref[...] = jnp.concatenate(denoms, axis=1)


def score_constants(size):
    return {"factor": size**-0.5 / math.log(2.0), "offset": 3.0 * size**0.5 / math.log(2.0)}


def attend(query, keys, base, values, size):
    rows, width = query.shape[0], values.shape[1]
    block = math.gcd(rows, 256)
    return pl.pallas_call(
        functools.partial(attend_body, size=size, base=base, **score_constants(size)),
        grid=(rows // block,),
        in_specs=[row_spec(block, query.shape[1]), full_spec(keys.shape), full_spec(values.shape)],
        out_specs=[row_spec(block, width)] * 2,
        out_shape=[struct((rows, width), F32)] * 2,
        name="attend",
    )(query, keys, values)


def attend_text_body(
    order_ref,
    query_ref,
    key_ref,
    value_ref,
    keep_ref,
    gate_ref,
    own_ref,
    mixed_ref,
    cross_ref,
    denom_ref,
    *,
    size,
    factor,
    offset,
):
    rows, width = cross_ref.shape
    part_rows = mixed_ref.shape[1]
    keep = keep_ref[...]
    outs, denoms = [], []
    for part in head_parts(width, size):
        wts = weights_of(query_ref[:, part], key_ref[:, part], factor, offset) * keep
        denom = jnp.sum(wts, axis=1, keepdims=True)
        outs.append(dot(wts.astype(BF16), value_ref[:, part]) / denom)
        denoms.append(jnp.broadcast_to(denom, (rows, size)))
    cross = jnp.concatenate(outs, axis=1)
    cross_ref[...], denom_ref[...] = cross, jnp.concatenate(denoms, axis=1)
    mixed = (own_ref[...] + gate_ref[...] * cross).astype(BF16)
    first = pl.program_id(0) * (rows // part_rows)
    for index in range(rows // part_rows):
        mixed_ref[order_ref[first + index]] = mixed[index * part_rows : (index + 1) * part_rows]


def attend_text(order, query, text_key, text_value, keep, gate, own, size):
    rows, width = own.shape
    slots, count = text_key.shape[0], order.shape[0]
    part_rows = rows // count
    block = part_rows * math.gcd(count, max(1, 512 // part_rows))
    return pl.pallas_call(
        functools.partial(attend_text_body, size=size, **score_constants(size)),
        grid_spec=pltpu.PrefetchScalarGridSpec(
            num_scalar_prefetch=1,
            grid=(rows // block,),
            in_specs=[
                row_spec(block, query.shape[1]),
                full_spec((slots, width)),
                full_spec((slots, width)),
                full_spec((1, slots)),
                full_spec((1, width)),
                row_spec(block, width),
            ],
            out_specs=[full_spec((count, part_rows, width))] + [row_spec(block, width)] * 2,
        ),
        out_shape=[struct((count, part_rows, width), BF16)] + [struct((rows, width), F32)] * 2,
        name="attend_text",
    )(order, query, text_key, text_value, keep[None], gate[None], own)


def attend_back_body(
    order_ref, query_ref, out_ref, denom_ref, dmixed_ref, key_ref, value_ref, *refs, size, base, factor, offset, text
):
    if text:
        keep_ref, gate_ref, dquery_ref, dkey_ref, dvalue_ref, dgate_ref = refs
    else:
        start_ref, dquery_ref, dkey_ref, dvalue_ref = refs
    rows, width = out_ref.shape
    part_rows = dmixed_ref.shape[1]
    step = pl.program_id(0)
    first = step * (rows // part_rows)
    dmixed = jnp.concatenate(
        [dmixed_ref[order_ref[first + index]] for index in range(rows // part_rows)], axis=0
    ).astype(F32)
    out, inv = out_ref[...], 1.0 / denom_ref[...]

    @pl.when(step == 0)
    def _():
        dkey_ref[...] = jnp.zeros_like(dkey_ref)
        dvalue_ref[...] = jnp.zeros_like(dvalue_ref)
        if text:
            dgate_ref[...] = jnp.zeros_like(dgate_ref)

    if text:
        dgate_ref[...] += jnp.sum(dmixed * out, axis=0, keepdims=True)
        dmixed = dmixed * gate_ref[...]
    dnumer = (dmixed * inv).astype(BF16)
    level = -(dmixed * out * inv)
    scale = size**-0.5
    results = []
    for part in head_parts(width, size):
        query, numer = query_ref[:, part], dnumer[:, part]
        keys = key_ref[:, base + part.start : base + part.stop]
        column = jnp.sum(level[:, part], axis=1, keepdims=True)
        level_row = jnp.broadcast_to(column, (rows, 128)).T[:1]
        wts = weights_of(keys, query, factor, offset)
        if text:
            wts = wts * keep_ref[...]
        dwts = lax.dot_general(
            value_ref[:, part], numer, (((1,), (1,)), ((), ())), preferred_element_type=F32
        )
        dscores = (wts * (dwts + level_row)).astype(BF16)
        dquery = (dot(keys.T, dscores) * scale).T
        results.append((dquery, dot(dscores, query) * scale, dot(wts.astype(BF16), numer)))
    dquery, dkey, dvalue = (jnp.concatenate(heads, axis=1) for heads in zip(*results))
    dquery_ref[...] = dquery if text else dquery + start_ref[...]
    dkey_ref[...] += dkey
    dvalue_ref[...] += dvalue


def attend_back(order, query, out, denom, dmixed, keys, base, values, size, text=None, start=None):
    rows, width = out.shape
    slots = keys.shape[0]
    part_rows = rows // order.shape[0]
    block = part_rows * math.gcd(order.shape[0], max(1, (256 if text is None else 512) // part_rows))
    if text is None:
        extra, extra_specs, ends = (start,), [row_spec(block, width)], []
    else:
        extra, ends = (text[0][:, None], text[1][None]), [(1, width)]
        extra_specs = [full_spec((slots, 1)), full_spec((1, width))]
    return pl.pallas_call(
        functools.partial(
            attend_back_body, size=size, base=base, text=text is not None, **score_constants(size)
        ),
        grid_spec=pltpu.PrefetchScalarGridSpec(
            num_scalar_prefetch=1,
            grid=(rows // block,),
            in_specs=[row_spec(block, query.shape[1]), row_spec(block, width), row_spec(block, width)]
            + [full_spec(dmixed.shape), full_spec(keys.shape), full_spec(values.shape)]
            + extra_specs,
            out_specs=[row_spec(block, width)]
            + [full_spec(values.shape)] * 2
            + [full_spec(shape) for shape in ends],
        ),
        out_shape=[struct((rows, width), F32)]
        + [struct(values.shape, F32)] * 2
        + [struct(shape, F32) for shape in ends],
        name="text_back" if text else "attend_back",
    )(order, query, out, denom, dmixed, keys, values, *extra)


def norm_heads_back(raw, upstream, gain, size):
    gain_grad, grads = 0.0, []
    for part in head_parts(raw.shape[1], size):
        head, grad = raw[:, part], upstream[part.start // size]
        inv = inverse_rms(head)
        hat = head * inv
        gain_grad = gain_grad + jnp.sum(grad * hat, axis=0, keepdims=True)
        scaled = grad * gain
        grads.append(inv * (scaled - hat * jnp.mean(scaled * hat, axis=1, keepdims=True)))
    return gain_grad, jnp.concatenate(grads, axis=1)


def finish_body(
    raw_ref, dquery_ref, dkey_ref, dvalue_ref, cos_ref, sin_ref, gain_ref, means_ref, swaps_ref, out_ref, dgain_ref
):
    width = gain_ref.shape[1]

    @pl.when(pl.program_id(0) == 0)
    def _():
        dgain_ref[...] = jnp.zeros_like(dgain_ref)

    raw, means = raw_ref[:, :width], means_ref[...]
    inv = lax.rsqrt(exact_dot(raw * raw, means) + EPSILON)
    hat = raw * inv
    grad = jnp.concatenate([dquery_ref[...], dkey_ref[...].astype(F32)], axis=1)
    swapped = exact_dot(grad, swaps_ref[...])
    grad = grad * widen(cos_ref[...], width) - swapped * widen(sin_ref[...], width)
    dgain_ref[...] += jnp.sum(grad * hat, axis=0, keepdims=True)
    scaled = grad * gain_ref[...]
    out = inv * (scaled - hat * exact_dot(scaled * hat, means))
    out_ref[...] = jnp.concatenate([out.astype(BF16), dvalue_ref[...].astype(BF16)], axis=1)


def finish(raw, dquery, dkey, dvalue, cosine, sine, gain, size):
    rows, width = raw.shape[0], gain.shape[0]
    block = math.gcd(rows, 256)
    return pl.pallas_call(
        finish_body,
        grid=(rows // block,),
        in_specs=[row_spec(block, raw.shape[1])]
        + [row_spec(block, width // 2)] * 3
        + [row_spec(block, cosine.shape[1])] * 2
        + [full_spec((1, width)), full_spec((width, width)), full_spec((width, width))],
        out_specs=[row_spec(block, raw.shape[1]), full_spec((1, width))],
        out_shape=[struct(raw.shape, BF16), struct((1, width), F32)],
        name="finish",
    )(raw, dquery, dkey, dvalue, cosine, sine, gain[None], head_means(width, size), half_swaps(width, size))


def finish_text_body(raw_ref, dkey_ref, dvalue_ref, gain_in_ref, out_ref, gain_ref):
    width, size = dkey_ref.shape[1], gain_in_ref.shape[1]
    upstream = [dkey_ref[:, part] for part in head_parts(width, size)]
    gain_ref[...], grads = norm_heads_back(raw_ref[:, :width], upstream, gain_in_ref[...], size)
    out_ref[...] = jnp.concatenate([grads.astype(BF16), dvalue_ref[...].astype(BF16)], axis=1)


def finish_text(raw, dkey, dvalue, gain):
    return pl.pallas_call(
        finish_text_body,
        out_shape=[struct(raw.shape, BF16), struct((1, gain.shape[0]), F32)],
        name="finish_text",
    )(raw, dkey, dvalue, gain[None])


def join_body(parts_ref, *outs, width):
    for index, out_ref in enumerate(outs):
        for turn_index in range(parts_ref.shape[0]):
            at = turn_index * width
            out_ref[:, at : at + width] = parts_ref[turn_index, :, index * width : (index + 1) * width].astype(F32)


def join_heads(parts, width):
    count, rows, total = parts.shape
    return pl.pallas_call(
        functools.partial(join_body, width=width),
        out_shape=[struct((rows, count * width), F32)] * (total // width),
        name="join_heads",
    )(parts)


def join_groups_body(parts_ref, *outs, groups, width):
    count = parts_ref.shape[0]
    for index, out_ref in enumerate(outs):
        for group in range(groups):
            for turn_index in range(count):
                at = (group * count + turn_index) * width
                source = (index * groups + group) * width
                out_ref[:, at : at + width] = parts_ref[turn_index, :, source : source + width].astype(F32)


def join_groups(parts, groups, width, kinds):
    count, rows, _ = parts.shape
    return pl.pallas_call(
        functools.partial(join_groups_body, groups=groups, width=width),
        out_shape=[struct((rows, groups * count * width), F32)] * kinds,
        name="join_groups",
    )(parts)


def split_heads_body(*refs, width):
    *ins, out_ref = refs
    for index, in_ref in enumerate(ins):
        for device in range(out_ref.shape[0]):
            at = device * width
            out_ref[device, :, index * width : (index + 1) * width] = in_ref[:, at : at + width]


def split_heads(weights, count):
    rows, columns = weights[0].shape
    width = columns // count
    return pl.pallas_call(
        functools.partial(split_heads_body, width=width),
        out_shape=struct((count, rows, len(weights) * width), BF16),
        name="split_heads",
    )(*weights)


def split_groups_body(*refs, groups, width):
    *ins, out_ref = refs
    count = out_ref.shape[0]
    for index, in_ref in enumerate(ins):
        for group in range(groups):
            for device in range(count):
                at, to = (group * count + device) * width, (index * groups + group) * width
                out_ref[device, :, to : to + width] = in_ref[:, at : at + width]


def split_groups(weights, count, groups, width):
    rows = weights[0].shape[0]
    return pl.pallas_call(
        functools.partial(split_groups_body, groups=groups, width=width),
        out_shape=struct((count, rows, len(weights) * groups * width), BF16),
        name="split_groups",
    )(*weights)


def take_columns_body(order_ref, in_ref, *outs, groups, count, width):
    for index, out_ref in enumerate(outs):
        for group in range(groups):
            at = pl.multiple_of((group * count + order_ref[index]) * width, width)
            out_ref[:, group * width : (group + 1) * width] = in_ref[:, pl.ds(at, width)]


def take_columns(values, order, takers, groups, count, width):
    rows = values.shape[0]
    if width % 128:
        split = values.reshape(rows, groups, count, width)
        return [pick(split, order[at], 2).reshape(rows, groups * width) for at in range(takers)]
    return pl.pallas_call(
        functools.partial(take_columns_body, groups=groups, count=count, width=width),
        grid_spec=pltpu.PrefetchScalarGridSpec(
            num_scalar_prefetch=1,
            grid=(1,),
            in_specs=[full_spec(values.shape)],
            out_specs=[full_spec((rows, groups * width))] * takers,
        ),
        out_shape=[struct((rows, groups * width), values.dtype)] * takers,
        name="take_columns",
    )(order, values)


def head_grads_body(text_ref, dtext_ref, mod_ref, dqkv_ref, out_ref, *, factor):
    text = dot(text_ref[...], dtext_ref[...], 0, 0) * factor
    out_ref[:, : text.shape[1]] = text.astype(BF16)
    out_ref[:, text.shape[1] :] = dot(mod_ref[...], dqkv_ref[...], 0, 0).astype(BF16)


def head_grads(text, dtext, mod, dqkv, factor):
    width, total = text.shape[1], dtext.shape[1] + dqkv.shape[1]
    block = math.gcd(width, 256)
    return pl.pallas_call(
        functools.partial(head_grads_body, factor=factor),
        grid=(width // block,),
        in_specs=[
            pl.BlockSpec((text.shape[0], block), lambda i: (0, i)),
            full_spec(dtext.shape),
            pl.BlockSpec((mod.shape[0], block), lambda i: (0, i)),
            full_spec(dqkv.shape),
        ],
        out_specs=row_spec(block, total),
        out_shape=struct((width, total), BF16),
        name="head_grads",
    )(text, dtext, mod, dqkv)


def feed_body(*refs, count, steps):
    pieces = refs[:count]
    weight_ref, down_ref, dfeed_ref, mod_ref, inner_ref, dhidden_ref, buffer, sems = refs[count:]
    step, per = pl.program_id(0), count // steps
    rows, hidden = pieces[0].shape[0], inner_ref.shape[1]

    def fetch(at):
        for index in range(per):
            pltpu.make_async_copy(
                pieces[at * per + index], buffer.at[at % 2, pl.ds(index * rows, rows)], sems.at[at % 2, index]
            ).start()

    @pl.when(step == 0)
    def _():
        fetch(0)

    for at in range(steps - 1):

        @pl.when(step == at)
        def _(at=at):
            fetch(at + 1)

    slot = step % 2
    for index in range(per):
        pltpu.make_async_copy(
            pieces[0], buffer.at[slot, pl.ds(index * rows, rows)], sems.at[slot, index]
        ).wait()
    mod = buffer[slot]
    mod_ref[...] = mod
    gate = dot(mod, weight_ref[:, :hidden])
    up = dot(mod, weight_ref[:, hidden:])
    sigmoid = 1.0 / (1.0 + jnp.exp(-gate))
    silu = gate * sigmoid
    inner = (silu * up).astype(BF16)
    inner_ref[...] = inner
    dinner = dot(dfeed_ref[...], down_ref[...], 1, 1)
    dhidden_ref[:, :hidden] = (dinner * up * (sigmoid * (1.0 + gate * (1.0 - sigmoid)))).astype(BF16)
    dhidden_ref[:, hidden:] = (dinner * silu).astype(BF16)


def feed(pieces, weight, down, dfeed):
    count = len(pieces)
    rows, width = pieces[0].shape
    hidden = down.shape[0]
    steps = count // 2
    block = rows * 2
    return pl.pallas_call(
        functools.partial(feed_body, count=count, steps=steps),
        grid=(steps,),
        in_specs=[pl.BlockSpec(memory_space=pl.ANY)] * count
        + [
            full_spec(weight.shape),
            full_spec(down.shape),
            row_spec(block, width),
        ],
        out_specs=[
            row_spec(block, width),
            row_spec(block, hidden),
            row_spec(block, 2 * hidden),
        ],
        out_shape=[
            struct((count * rows, width), BF16),
            struct((count * rows, hidden), BF16),
            struct((count * rows, 2 * hidden), BF16),
        ],
        scratch_shapes=[pltpu.VMEM((2, block, width), BF16), pltpu.SemaphoreType.DMA((2, 2))],
        name="feed",
    )(*pieces, weight, down, dfeed)


def place_body(order_ref, *refs):
    *pieces, out_ref = refs
    for at, piece in enumerate(pieces):
        out_ref[:, order_ref[at]] = piece[...]


def place(pieces, order):
    groups, rows, columns = pieces[0].shape
    return pl.pallas_call(
        place_body,
        grid_spec=pltpu.PrefetchScalarGridSpec(
            num_scalar_prefetch=1,
            grid=(groups,),
            in_specs=[pl.BlockSpec((1, rows, columns), lambda i, *_: (i, 0, 0))] * len(pieces),
            out_specs=pl.BlockSpec((1, len(pieces), rows, columns), lambda i, *_: (i, 0, 0, 0)),
        ),
        out_shape=struct((groups, len(pieces), rows, columns), pieces[0].dtype),
        name="place",
    )(order, *pieces)


def modulate_body(*refs, count, own_rows):
    pieces = refs[:count]
    scale_ref, shift_ref, gate_ref, mod_ref, dfeed_ref, tail_ref, buffer, sems = refs[count:]
    step = pl.program_id(0)

    def fetch(at):
        pltpu.make_async_copy(pieces[at], buffer.at[at % 2], sems.at[at % 2]).start()

    @pl.when(step == 0)
    def _():
        fetch(0)

    for at in range(count - 1):

        @pl.when(step == at)
        def _(at=at):
            fetch(at + 1)

    slot = step % 2
    pltpu.make_async_copy(pieces[0], buffer.at[slot], sems.at[slot]).wait()
    tokens = buffer[slot, :own_rows].astype(F32)
    mod_ref[...] = (tokens * inverse_rms(tokens) * scale_ref[...] + shift_ref[...]).astype(BF16)
    dfeed_ref[...] = (buffer[slot, own_rows : 2 * own_rows].astype(F32) * gate_ref[...]).astype(BF16)
    tail_ref[0] = buffer[slot, 2 * own_rows :, : tail_ref.shape[2]]


def modulate(pieces, scale, shift, gate, own_rows, tail_width):
    count = len(pieces)
    rows, width = pieces[0].shape
    tail = (1, rows - 2 * own_rows, tail_width)
    return pl.pallas_call(
        functools.partial(modulate_body, count=count, own_rows=own_rows),
        grid=(count,),
        in_specs=[pl.BlockSpec(memory_space=pl.ANY)] * count + [full_spec((1, width))] * 3,
        out_specs=[row_spec(own_rows, width)] * 2 + [pl.BlockSpec(tail, lambda i: (i, 0, 0))],
        out_shape=[struct((count * own_rows, width), BF16)] * 2 + [struct((count,) + tail[1:], BF16)],
        scratch_shapes=[pltpu.VMEM((2, rows, width), BF16), pltpu.SemaphoreType.DMA((2,))],
        name="modulate",
    )(*pieces, scale[None], shift[None], gate[None])


def outer_body(order_ref, left_ref, right_ref, out_ref):
    groups, _, rows, inner = left_ref.shape
    product = dot(left_ref[...].reshape(groups * rows, inner), right_ref[...]).astype(BF16)
    out_ref[0] = product.reshape(out_ref.shape[1:])


def outer(left, right, order):
    groups, count, rows, inner = left.shape
    columns = right.shape[1]
    return pl.pallas_call(
        outer_body,
        grid_spec=pltpu.PrefetchScalarGridSpec(
            num_scalar_prefetch=1,
            grid=(count,),
            in_specs=[
                pl.BlockSpec((groups, 1, rows, inner), lambda i, order_ref: (0, order_ref[i], 0, 0)),
                full_spec((inner, columns)),
            ],
            out_specs=pl.BlockSpec((1, groups, rows, columns), lambda i, order_ref: (i, 0, 0, 0)),
        ),
        out_shape=struct((count, groups, rows, columns), BF16),
        name="outer",
    )(order, left, right)


def axes_size(axes):
    return math.prod(lax.axis_size(axis) for axis in axes)


def swap(x, axes, mask):
    return lax.ppermute(x, axes, [(i, i ^ mask) for i in range(axes_size(axes))])


def pick(x, index, axis=0):
    return lax.dynamic_index_in_dim(x, index, axis, keepdims=False)


def spread(x, axes, masks):
    first, second, fast = masks[1], masks[2], masks[4]
    half = x.shape[0] // 2
    one = swap(x, axes, first)
    two = swap(x, axes, second)
    far = jnp.concatenate([swap(two[:half], axes, first), swap(one[half:], axes, second)], axis=0)
    near = [x, one, two, far]
    return near + [swap(piece, axes, fast) for piece in near]


class Collect:
    def __init__(self, keep, send, axes, masks):
        self.axes, self.masks, self.keep = axes, masks, keep
        self.got = swap(send, axes, masks[4])

    def exchange(self, x, index):
        return swap(x.astype(BF16), self.axes, self.masks[index])

    def part(self, slots, columns):
        return self.keep[slots, :, columns].astype(F32) + self.got[slots, :, columns].astype(F32)

    def first(self):
        half = self.keep.shape[2] // 2
        left, right = slice(0, half), slice(half, 2 * half)
        self.left_got = self.exchange(self.part(slice(1, 4, 2), left), 1)
        self.right_got = self.exchange(self.part(slice(2, 4), right), 2)
        self.left = [self.part(0, left), self.part(2, left)]
        self.right = [self.part(0, right), self.part(1, right)]

    def second(self):
        left_got, right_got = self.left_got.astype(F32), self.right_got.astype(F32)
        self.left_end = self.exchange(self.left[1] + left_got[1], 2)
        self.right_end = self.exchange(self.right[1] + right_got[1], 1)

    def end(self):
        left = self.left[0] + self.left_got[0].astype(F32) + self.left_end.astype(F32)
        right = self.right[0] + self.right_got[0].astype(F32) + self.right_end.astype(F32)
        return jnp.concatenate([left, right], axis=1)

    def tie_first(self, *others):
        self.got, *rest = tie(self.got, *others)
        self.first()
        return rest

    def tie_second(self, *others):
        self.left_got, self.right_got, *rest = tie(self.left_got, self.right_got, *others)
        self.second()
        return rest

    def tie_end(self, *others):
        self.left_end, self.right_end, *rest = tie(self.left_end, self.right_end, *others)
        return [self.end()] + rest


def tie(*values):
    return lax.optimization_barrier(values)


def halves_product(left, right, right_dim, count):
    middle = left.shape[0] // 2
    shape = (count // 2, left.shape[0] // count, right.shape[1 - right_dim])
    send = dot(left[middle:], right, 1, right_dim).astype(BF16).reshape(shape)
    send, first = tie(send, left[:middle])
    return dot(first, right, 1, right_dim).astype(BF16).reshape(shape), send


def small_sum(x, axes):
    count = axes_size(axes)
    if count > 8 or count & (count - 1):
        return lax.psum(x, axes)
    total = x
    for mask in range(1, count):
        total = total + swap(x, axes, mask)
    return total


def partner_sum(parts, axes):
    total = parts[0].astype(F32)
    for mask in range(1, len(parts)):
        total = total + swap(parts[mask], axes, mask).astype(F32)
    return total


def partner_spread(x, axes):
    return [swap(x, axes, mask) if mask else x for mask in range(axes_size(axes))]


def turn_spread(x, axes):
    return turn(jnp.broadcast_to(x, (axes_size(axes),) + x.shape), axes)


def turn_sum(parts, axes):
    return jnp.sum(turn(parts, axes).astype(F32), axis=0)


def turn(x, axes):
    return lax.all_to_all(x, axes, split_axis=0, concat_axis=0, tiled=False)


def on_device(
    tokens,
    positions,
    captions,
    caption_lengths,
    conditioning,
    modulation_weight,
    modulation_bias,
    attention_gain,
    query_weight,
    key_weight,
    value_weight,
    query_gain,
    key_gain,
    text_weight,
    textkey_weight,
    textvalue_weight,
    textkey_gain,
    cross_gate,
    output_weight,
    feedforward_gain,
    gate_weight,
    up_weight,
    down_weight,
    cotangent,
):
    wide_count, narrow_count = lax.axis_size(W), lax.axis_size(N)
    clip_count = lax.axis_size(C)
    clip_index, wide_index = lax.axis_index(C), lax.axis_index(W)
    own_rows, model_width = tokens.shape[1], tokens.shape[2]
    head_size = query_gain.shape[0]
    head_count = model_width // head_size
    score_scale = head_size ** (-0.5)
    score_shift = 3.0 * math.sqrt(head_size)
    split_tokens = head_count % (wide_count * narrow_count) != 0
    tp, dp = ((N,), (C, W)) if split_tokens else (PLANE, (C,))
    tp_count, dp_count = axes_size(tp), axes_size(dp)
    tp_index = lax.axis_index(tp)
    masks = [0, 1, 4, 5, 2, 3, 6, 7]
    order = (tp_index ^ jnp.array(masks, jnp.int32)).astype(jnp.int32)
    clip_order = (clip_index ^ jnp.arange(clip_count, dtype=jnp.int32)).astype(jnp.int32)
    group_rows = own_rows * tp_count
    local_heads = head_count // tp_count
    head_width = local_heads * head_size
    weight_rows = query_weight.shape[0]
    hidden_rows, hidden_width = down_weight.shape[0], gate_weight.shape[1]
    local_hidden = hidden_width // tp_count

    text_rows, caption_rows = text_weight.shape[0], captions.shape[1]
    slot_count = caption_rows * narrow_count
    slot_part = slot_count // tp_count

    def gather_rows(rows):
        return lax.all_gather(rows, dp, axis=0, tiled=True)

    def scatter_rows(grads):
        return lax.psum_scatter(grads, dp, scatter_dimension=0, tiled=True)

    row_stack = gather_rows(jnp.concatenate([output_weight, text_weight], axis=0))
    row_stack = row_stack.reshape(dp_count, weight_rows + text_rows, model_width)

    head_parts_in = split_heads((textkey_weight, textvalue_weight, query_weight, key_weight, value_weight), tp_count)
    place_rows = jnp.stack([positions[0] // 64, positions[0] % 64]).astype(BF16)
    place_rows = jnp.pad(place_rows, ((0, 30), (0, model_width - own_rows)))
    bundle = jnp.concatenate([tokens[0], cotangent[0], place_rows], axis=0)
    head_parts_got = turn(head_parts_in, tp)
    head_slice = gather_rows(head_parts_got.reshape(tp_count * weight_rows, 5 * head_width))
    text_slice, qkv_slice = head_slice[:, : 2 * head_width], head_slice[:, 2 * head_width :]

    cond_float = conditioning.astype(F32)
    cond_act = jax.nn.silu(cond_float)
    cond_rows = jnp.stack([pick(cond_act, clip_order[at]) for at in range(clip_count)])
    weight_float = modulation_weight.astype(F32)
    partial_mod = jnp.dot(cond_rows, weight_float, precision=HIGHEST, preferred_element_type=F32)
    clip_mod = partner_sum([partial_mod[at] for at in range(clip_count)], (C,))
    own_mod = small_sum(clip_mod, PLANE) + modulation_bias
    own_mod, bundle = tie(own_mod, bundle)
    pieces = spread(bundle, tp, masks)
    shift_attn, scale_attn, gate_attn, shift_feed, scale_feed, gate_feed = jnp.split(own_mod, 6)

    hidden_in = split_groups((gate_weight, up_weight), tp_count, dp_count, hidden_rows)
    pieces[3], hidden_in = tie(pieces[3], hidden_in)
    hidden_parts, down_rows = tie(turn(hidden_in, tp), down_weight)
    hidden_slice = gather_rows(hidden_parts.reshape(tp_count * weight_rows, 2 * local_hidden))
    down_slice = gather_rows(down_rows)

    caption_sent = take_columns(captions[0], tp_index ^ jnp.arange(narrow_count), narrow_count, dp_count, tp_count, text_rows)
    caption_got = [swap(part, (N,), at) if at else part for at, part in enumerate(caption_sent)]
    narrow_order = (lax.axis_index(N) ^ jnp.arange(narrow_count, dtype=jnp.int32)).astype(jnp.int32)
    caption_columns = place([part[None] for part in caption_got], narrow_order).reshape(slot_count, -1)

    mod_in, dfeed, tails = modulate(
        pieces, attention_gain * (1.0 + scale_attn), shift_attn, gate_feed, own_rows, own_rows
    )
    position_all = (tails[:, 0].astype(F32) * 64.0 + tails[:, 1].astype(F32)).reshape(group_rows)
    cosine, sine = rope_tables(position_all, head_size, 2 * head_size)
    head_gain = jnp.concatenate([jnp.tile(query_gain, local_heads), jnp.tile(key_gain, local_heads)])

    output_rows = row_stack[:, :weight_rows].reshape(dp_count * weight_rows, model_width)
    text_own_rows = row_stack[:, weight_rows:].reshape(-1, model_width)
    text_parts = dot(caption_columns, text_own_rows).astype(BF16).reshape(tp_count, slot_part, model_width)
    text_own = turn_sum(text_parts, tp).astype(BF16)
    text_proj = turn_spread(text_own, tp).reshape(slot_count, model_width)
    output_pieces = [
        piece.reshape(dp_count, weight_rows, model_width) for piece in spread(output_rows, tp, masks)
    ]
    output_full = place(output_pieces, order).reshape(model_width, model_width)

    qkv_raw = dot(mod_in, qkv_slice)
    heads, value_own = prepare(qkv_raw, cosine, sine, head_gain, head_size)
    if split_tokens:
        keys_all, key_base = lax.all_gather(heads[:, head_width:], W, axis=0, tiled=True), 0
        values_all = lax.all_gather(value_own, W, axis=0, tiled=True)
    else:
        keys_all, values_all, key_base = heads, value_own, head_width
    own_out, denom = attend(heads, keys_all, key_base, values_all, head_size)
    keep = (jnp.arange(slot_count) < caption_lengths[clip_index]).astype(F32)
    text_raw = dot(text_proj, text_slice)
    text_key, text_value = prepare_text(text_raw, textkey_gain, head_width)
    text_gate = pick(jnp.tanh(cross_gate).reshape(tp_count, local_heads), tp_index)
    gate_lanes = jnp.repeat(text_gate, head_size)
    mixed, cross_out, text_denom = attend_text(
        order, heads, text_key, text_value, keep, gate_lanes, own_out, head_size
    )

    token_float = tokens[0].astype(F32)
    inv_attn = inverse_rms(token_float)
    hat_attn = token_float * inv_attn
    normed_attn = hat_attn * attention_gain
    mixed_own = turn(mixed, tp).transpose(1, 0, 2).reshape(own_rows, model_width)
    attn_out = dot(mixed_own, output_full)
    resid = token_float + gate_attn * attn_out
    inv_feed = inverse_rms(resid)
    hat_feed = resid * inv_feed
    normed_feed = hat_feed * feedforward_gain
    mod_own = (normed_feed * (1.0 + scale_feed) + shift_feed).astype(BF16)

    mod_ff, inner, dhidden = feed(spread(mod_own, tp, masks), hidden_slice, down_slice, dfeed)
    dmod_sum = Collect(*halves_product(dhidden, hidden_slice, 1, tp_count), tp, masks)
    dmod_sum.keep, mod_ff, dhidden = tie(dmod_sum.keep, mod_ff, dhidden)
    dmod_sum.first()
    dhidden_grads = dot(mod_ff, dhidden, 0, 0).astype(BF16)
    (dhidden_grads,) = dmod_sum.tie_second(dhidden_grads)
    ddown_grads = dot(inner, dfeed, 0, 0).astype(BF16)
    dmod_ff, ddown_grads = dmod_sum.tie_end(ddown_grads)
    dhidden_rows = scatter_rows(dhidden_grads)
    downweight_grad = scatter_rows(ddown_grads).astype(F32)

    dout = cotangent[0].astype(F32)
    dshift_feed = jnp.sum(dmod_ff, axis=0)
    dscale_feed = jnp.sum(dmod_ff * normed_feed, axis=0)
    dfeed_gain, dresid_norm = norm_backward(
        hat_feed, inv_feed, feedforward_gain, dmod_ff * (1.0 + scale_feed)
    )
    dresid = dout + dresid_norm
    dgate_attn = jnp.sum(dresid * attn_out, axis=0)
    dattn = (gate_attn * dresid).astype(BF16)

    dmixed_own = dot(dattn, output_full, 1, 1).astype(BF16)
    dmixed_own, inner, mixed_own = tie(dmixed_own, inner, mixed_own)
    dmixed = turn(dmixed_own.reshape(own_rows, tp_count, head_width).transpose(1, 0, 2), tp)
    feed_sum = Collect(*halves_product(inner, down_slice, 0, tp_count), tp, masks)
    feed_sum.keep, mixed_own = tie(feed_sum.keep, mixed_own)
    dout_parts = outer(
        mixed_own.T.reshape(dp_count, tp_count, weight_rows, own_rows), dattn, order
    ).reshape(tp_count, dp_count * weight_rows, model_width)
    dmixed, dout_parts = tie(dmixed, dout_parts)
    out_sum = Collect(dout_parts[: tp_count // 2], dout_parts[tp_count // 2 :], tp, masks)
    (dmixed,) = feed_sum.tie_first(dmixed)
    dquery_text, dtext_key, dtext_value, dgate_lanes = attend_back(
        order, heads, cross_out, text_denom, dmixed, text_key, 0, text_value, head_size, text=(keep, gate_lanes)
    )
    if split_tokens:
        dtext_key, dtext_value = lax.psum((dtext_key, dtext_value), W)
    dtext_heads, dtkey_gain = finish_text(text_raw, dtext_key, dtext_value, textkey_gain)
    dtext_parts = dot(dtext_heads, text_slice, 1, 1).astype(BF16).reshape(tp_count, slot_part, model_width)
    dtext_parts, dquery_text = tie(dtext_parts, dquery_text)
    dtext_turned = turn(dtext_parts, tp)
    (dquery_text,) = feed_sum.tie_second(dquery_text)
    shared = 1.0 / wide_count if split_tokens else 1.0
    dquery, dkey, dvalue = attend_back(
        order, heads, own_out, denom, dmixed, keys_all, key_base, values_all, head_size, start=dquery_text
    )
    dtext_turned, dquery = tie(dtext_turned, dquery)
    dtext_own = jnp.sum(dtext_turned.astype(F32), axis=0).astype(BF16)
    dtext_all = turn_spread(dtext_own, tp).reshape(slot_count, model_width)
    if split_tokens:
        dkey = lax.psum_scatter(dkey.astype(BF16), W, scatter_dimension=0, tiled=True)
        dvalue = lax.psum_scatter(dvalue.astype(BF16), W, scatter_dimension=0, tiled=True)
    dcross_gate = jnp.sum(dgate_lanes.reshape(local_heads, head_size), axis=1) * (1.0 - text_gate * text_gate)
    (dquery,) = out_sum.tie_first(dquery)
    dqkv, dhead_gain = finish(qkv_raw, dquery, dkey, dvalue, cosine, sine, head_gain, head_size)
    (dqkv,) = out_sum.tie_second(dqkv)

    middle = group_rows // 2
    shape = (tp_count // 2, own_rows, model_width)
    din_send = dot(dqkv[middle:], qkv_slice, 1, 1).astype(BF16).reshape(shape)
    dhidden_parts = turn(dhidden_rows.reshape(tp_count, weight_rows, 2 * local_hidden), tp)
    din_send, dqkv, dhidden_parts = tie(din_send, dqkv, dhidden_parts)
    dhead_grads = head_grads(text_proj, dtext_heads, mod_in, dqkv, shared)
    dhead_grads, dqkv = tie(dhead_grads, dqkv)
    dhead_rows = scatter_rows(dhead_grads)
    din_sum = Collect(dot(dqkv[:middle], qkv_slice, 1, 1).astype(BF16).reshape(shape), din_send, tp, masks)
    din_sum.first()
    feed_out, dtext_all = feed_sum.tie_end(dtext_all)
    dtext_grads = (dot(caption_columns, dtext_all, 0, 0) * shared).astype(BF16)
    textweight_grad = scatter_rows(dtext_grads).astype(F32)
    dcaption = dot(dtext_all, text_own_rows, 1, 1).astype(BF16).reshape(narrow_count, caption_rows, -1)
    (dcaption,) = din_sum.tie_second(dcaption)
    dmod_in = din_sum.end()

    dshift_attn = jnp.sum(dmod_in, axis=0)
    dscale_attn = jnp.sum(dmod_in * normed_attn, axis=0)
    dattn_gain, dtokens_norm = norm_backward(
        hat_attn, inv_attn, attention_gain, dmod_in * (1.0 + scale_attn)
    )
    tokens_grad = dresid + dtokens_norm
    block_output = resid + gate_feed * feed_out
    dgate_feed = jnp.sum(dout * feed_out, axis=0)
    head_range = jnp.arange(head_count) - tp_index * local_heads
    dgate_rows = jnp.sum(
        jnp.where(head_range[:, None] == jnp.arange(local_heads)[None, :], dcross_gate[None, :], 0.0), axis=1
    )
    dgains = jnp.sum(dhead_gain.reshape(2, local_heads, head_size), axis=1)
    pad = -head_count % head_size
    small = jnp.concatenate(
        [
            dshift_attn,
            dscale_attn,
            dgate_attn,
            dshift_feed,
            dscale_feed,
            dgate_feed,
            dattn_gain,
            dfeed_gain,
            dgains[0],
            dgains[1],
            dtkey_gain[0] * shared,
            dgate_rows,
            jnp.zeros((pad,), F32),
        ]
    )
    clip_small = jnp.stack(partner_spread(small_sum(small, PLANE), (C,)))
    mod_width = 6 * model_width
    dmod_all = clip_small[:, :mod_width]
    gains = jnp.sum(clip_small[:, mod_width:], axis=0)
    attngain_grad, feedgain_grad = gains[:model_width], gains[model_width : 2 * model_width]
    rest = gains[2 * model_width :]
    querygain_grad, keygain_grad, textgain_grad = (
        rest[:head_size],
        rest[head_size : 2 * head_size],
        rest[2 * head_size : 3 * head_size],
    )
    crossgate_grad = rest[3 * head_size : 3 * head_size + head_count]
    modweight_grad = jnp.dot(cond_rows.T, dmod_all, precision=HIGHEST, preferred_element_type=F32)
    dcond_rows = jnp.dot(dmod_all, weight_float.T, precision=HIGHEST, preferred_element_type=F32)
    dcond_act = jnp.stack([pick(dcond_rows, clip_order[at]) for at in range(clip_count)])
    sigmoid_cond = jax.nn.sigmoid(cond_float)
    conditioning_grad = dcond_act * sigmoid_cond * (1.0 + cond_float * (1.0 - sigmoid_cond))
    modbias_grad = jnp.sum(dmod_all, axis=0)

    dcaption_sent = jnp.broadcast_to(dcaption, (tp_count // narrow_count,) + dcaption.shape)
    dcaption_got = turn(dcaption_sent.reshape(tp_count, caption_rows, -1), tp)
    (captions_grad,) = join_groups(dcaption_got, dp_count, text_rows, 1)

    dout_group = out_sum.end().astype(BF16).reshape(dp_count, weight_rows, model_width)
    if split_tokens:
        outweight_grad = lax.psum_scatter(dout_group, dp, scatter_dimension=0, tiled=False).astype(F32)
    else:
        outweight_grad = partner_sum([pick(dout_group, clip_order[at]) for at in range(dp_count)], dp)
    gateweight_grad, upweight_grad = join_groups(dhidden_parts, dp_count, hidden_rows, 2)
    dhead_parts = turn(dhead_rows.reshape(tp_count, weight_rows, 5 * head_width), tp)
    textkey_grad, textvalue_grad, queryweight_grad, keyweight_grad, valueweight_grad = join_heads(
        dhead_parts, head_width
    )
    return (
        block_output[None],
        tokens_grad[None],
        captions_grad[None],
        conditioning_grad,
        modweight_grad,
        modbias_grad,
        attngain_grad,
        queryweight_grad,
        keyweight_grad,
        valueweight_grad,
        querygain_grad,
        keygain_grad,
        textweight_grad,
        textkey_grad,
        textvalue_grad,
        textgain_grad,
        crossgate_grad,
        outweight_grad,
        feedgain_grad,
        gateweight_grad,
        upweight_grad,
        downweight_grad,
    )


def solution(mesh):
    rows, whole = P(ALL, None), P()
    tokens, captions = P(C, PLANE, None), P(C, N, None)
    columns = P(None, ALL)
    return jax.shard_map(
        on_device,
        mesh=mesh,
        in_specs=(
            tokens,
            P(C, PLANE),
            captions,
            whole,
            columns,
            rows,
            whole,
            whole,
            rows,
            rows,
            rows,
            whole,
            whole,
            rows,
            rows,
            rows,
            whole,
            whole,
            rows,
            whole,
            rows,
            rows,
            rows,
            tokens,
        ),
        out_specs=(
            tokens,
            tokens,
            captions,
            columns,
            rows,
            whole,
            whole,
            rows,
            rows,
            rows,
            whole,
            whole,
            rows,
            rows,
            rows,
            whole,
            whole,
            rows,
            whole,
            rows,
            rows,
            rows,
        ),
        check_vma=False,
    )
```

time: 867 us -> 552 us (0.64)
  Pallas kernels: 304 us -> 110 us
  local copies, waits for them, and re-layouts: 85.8 us -> 39.8 us
  starting transfers between devices: 137 us -> 114 us
  matrix products: 79.3 us -> 58.5 us
  other arithmetic: 66.5 us -> 49.7 us
  blocking collectives: 0 us -> 15.2 us
  between operations: 38.5 us -> 23.3 us
  waiting for transfers between devices: 147 us -> 133 us
    pallas_call x2, Pallas kernels: 242 us -> 8.13 us  [place(): pl.pallas_call(place_body, grid_spec=pltpu.PrefetchScalarGridSpec(num_sca...]
    pallas_call x5 -> x13, Pallas kernels: 35.9 us -> 81.5 us  [the longest x2 21.1 us: attend_back(): pl.pallas_call(functools.partial(attend_back_body, size=size, base=base,...]
    unnamed x172 -> x147, local copies, waits for them, and re-layouts: 31.3 us -> 7.92 us
    all_to_all x12 -> x10, waiting for transfers between devices: 32.1 us -> 10.9 us  [turn(): return lax.all_to_all(x, axes, split_axis=0, concat_axis=0, tiled=False)]
    dot_general x21 -> x16, matrix products: 75.6 us -> 55.4 us  [dot(): lax.dot_general(left, right, (((left_dim,), (right_dim,)), ((), ())), pre...]
    all_to_all x0 -> x1, blocking collectives: none -> 15.2 us  [turn(): return lax.all_to_all(x, axes, split_axis=0, concat_axis=0, tiled=False)]
    ppermute x87 -> x68, starting transfers between devices: 85.7 us -> 72.8 us  [swap(): lax.ppermute(x, axes, [(i, i ^ mask) for i in range(axes_size(axes))])]
    reshape x14 -> x1, local copies, waits for them, and re-layouts: 12 us -> 0.08 us  [on_device(): dgains = jnp.sum(dhead_gain.reshape(2, local_heads, head_size), axis=1)]
  transfers between devices with their start and end apart: 106 -> 86, of which waited for: 36 -> 37; matrix products, arithmetic and copies ran while one was open for 25% -> 25% of each run, Pallas kernels for 35% -> 18%
where the time goes in v2:
time: 552 us; the launch traced here: 543 us
  waiting for transfers between devices  133 us (24%)
  starting transfers between devices  114 us (21%)
  Pallas kernels  110 us (20%)
  matrix products  58.5 us (11%)
  other arithmetic  49.7 us (9%)
  local copies, waits for them, and re-layouts  39.8 us (7%)
  between operations  23.3 us (4%)
  blocking collectives  15.2 us (3%)
    ppermute x68, waiting for transfers between devices, swap(): lax.ppermute(x, axes, [(i, i ^ mask) for i in range(axes_size(axes))])  119 us
    ppermute x68, starting transfers between devices, swap(): lax.ppermute(x, axes, [(i, i ^ mask) for i in range(axes_size(axes))])  72.8 us
    dot_general x16, matrix products, dot(): lax.dot_general(left, right, (((left_dim,), (right_dim,)), ((), ())), pre...  55.4 us
    all_to_all x10, starting transfers between devices, turn(): return lax.all_to_all(x, axes, split_axis=0, concat_axis=0, tiled=False)  39.7 us
    pallas_call x2, Pallas kernels, attend_back(): pl.pallas_call(functools.partial(attend_back_body, size=size, base=base,...  21.1 us
    all_to_all x1, blocking collectives, turn(): return lax.all_to_all(x, axes, split_axis=0, concat_axis=0, tiled=False)  15.2 us
    convert_element_type x8, other arithmetic, exchange(): return swap(x.astype(BF16), self.axes, self.masks[index])  14.2 us
    pallas_call x1, Pallas kernels, feed(): pl.pallas_call(functools.partial(feed_body, count=count, steps=steps), gr...  11.1 us
  transfers between devices with their start and end apart: 86, of which 37 were waited for; matrix products, arithmetic and copies ran while one was open for 25% of the time, Pallas kernels for 18%

profile of v2, /device:TPU:0, one launch (start us, length us, event | category | flops | bytes accessed | tf_op | source)
XLA Modules:
  0.0 543.4 jit_solution(9399088403905346874)
XLA Ops:
  11.5 5.3 all-to-all-start
  52.0 20.4 %collective-permute-done.11.refs_2_ = bf16[288,1536]{1,0:T(8,128)(2,1)S(1)} collective-permute-done((bf16[288,1536]{1,0:T(8,128)(2,1)S(1)}, bf16[288,1536]{1,0:T(8,128)(2,1)S(1)}, u32[]{:S(2)}, u32[]{:S(2)}) %collective-permute-start.11) | collective-permute-done | bytes 884768 | tf_op jit(solution)/shard_map/ppermute | solution.py:650
  78.9 6.9 %collective-permute-done.12 = bf16[144,1536]{1,0:T(8,128)(2,1)S(1)} collective-permute-done((bf16[144,1536]{1,0:T(8,128)(2,1)}, bf16[144,1536]{1,0:T(8,128)(2,1)S(1)}, u32[]{:S(2)}, u32[]{:S(2)}) %collective-permute-start.12) | collective-permute-done | bytes 442400 | tf_op jit(solution)/shard_map/ppermute | solution.py:650
  90.2 15.2 %all_to_all.55 = bf16[8,48,1024]{2,1,0:T(8,128)(2,1)} all-to-all(bf16[8,48,1024]{2,1,0:T(8,128)(2,1)S(1)} %copy-done.14), channel_id=1, replica_groups=mesh['clip'=4,'wide'=4,'narrow'=2] {'wide','narrow'}, dimensions={0} | all-to-all | bytes 1572864 | tf_op jit(solution)/shard_map/all_to_all | solution.py:753
  129.5 9.4 %modulate.1 = (bf16[1024,1536]{1,0:T(8,128)(2,1)}, bf16[1024,1536]{1,0:T(8,128)(2,1)}, bf16[8,32,128]{2,1,0:T(8,128)(2,1)}) custom-call(bf16[288,1536]{1,0:T(8,128)(2,1)} %copy-done.7, bf16[288,1536]{1,0:T(8,128)(2,1)} %copy-done.20, bf16[288,1536]{1,0:T(8,128)(2,1)} %copy-done.19, bf16[288,1536]{1,0:T(8,128)(2,1)} %constant_dynamic-update-slice_fusion.refs_3_, ...), custom_call_target="tpu_custom_call" | custom-call | tf_op jit(solution)/shard_map/modulate/pallas_call | solution.py:609
  155.8 6.7 %fusion.2.raw_ref = f32[1024,576]{1,0:T(8,128)} fusion(bf16[1024,1536]{1,0:T(8,128)(2,1)} %get-tuple-element.111.mod_ref, bf16[1536,960]{1,0:T(8,128)(2,1)} %all-gather.5.cloned.1.call-done), kind=kOutput, calls=%fused_computation.14 | convolution fusion | flops 1811939328 | bytes 7471104 | tf_op jit(solution)/shard_map/dot_general | solution.py:22
  162.5 6.3 %prepare.1 = (bf16[1024,384]{1,0:T(8,128)(2,1)}, bf16[1024,192]{1,0:T(8,128)(2,1)}) custom-call(f32[1024,576]{1,0:T(8,128)} %fusion.2.raw_ref, f32[1024,128]{1,0:T(8,128)} %get-tuple-element.255.cos_ref, f32[1024,128]{1,0:T(8,128)} %get-tuple-element.254.sin_ref, f32[1,384]{1,0:T(1,128)} %broadcast_in_dim.95.gain_ref, ...), custom_call_target="tpu_custom_call" | custom-call | tf_op jit(solution)/shard_map/prepare/pallas_call | solution.py:97
  168.7 6.7 %attend.1 = (f32[1024,192]{1,0:T(8,128)}, f32[1024,192]{1,0:T(8,128)}) custom-call(bf16[1024,384]{1,0:T(8,128)(2,1)} %get-tuple-element.113.query_ref.key_ref, bf16[1024,384]{1,0:T(8,128)(2,1)} %get-tuple-element.113.query_ref.key_ref, bf16[1024,192]{1,0:T(8,128)(2,1)} %get-tuple-element.118.value_ref), custom_call_target="tpu_custom_call" | custom-call | tf_op jit(solution)/shard_map/attend/pallas_call | solution.py:154
  180.3 5.9 %attend_text.1 = (bf16[8,128,192]{2,1,0:T(8,128)(2,1)}, f32[1024,192]{1,0:T(8,128)}, f32[1024,192]{1,0:T(8,128)}) custom-call(s32[8]{0:T(128)} %broadcast_xor_fusion.order_ref, bf16[1024,384]{1,0:T(8,128)(2,1)} %get-tuple-element.113.query_ref.key_ref, bf16[256,192]{1,0:T(8,128)(2,1)} %get-tuple-element.116.key_ref, ...), custom_call_target="tpu_custom_call" | custom-call | tf_op jit(solution)/shard_map/attend_text/pallas_call | solution.py:202
  192.4 5.8 %place.3 = bf16[4,8,48,1536]{3,2,1,0:T(8,128)(2,1)} custom-call(s32[8]{0:T(128)} %broadcast_xor_fusion.order_ref, bf16[4,48,1536]{2,1,0:T(8,128)(2,1)} %copy-done.16, bf16[4,48,1536]{2,1,0:T(8,128)(2,1)} %bitcast.26.refs_1_, bf16[4,48,1536]{2,1,0:T(8,128)(2,1)} %bitcast.27.refs_2_, bf16[4,48,1536]{2,1,0:T(8,128)(2,1)} %bitcast.197, ...), custom_call_target="tpu_custom_call" | custom-call | tf_op jit(solution)/shard_map/place/pallas_call | solution.py:566
  206.7 9.4 %collective-permute-done.28.refs_2_ = bf16[128,1536]{1,0:T(8,128)(2,1)S(1)} collective-permute-done((bf16[128,1536]{1,0:T(8,128)(2,1)S(1)}, bf16[128,1536]{1,0:T(8,128)(2,1)S(1)}, u32[]{:S(2)}, u32[]{:S(2)}) %collective-permute-start.28) | collective-permute-done | bytes 393248 | tf_op jit(solution)/shard_map/ppermute | solution.py:650
  228.8 11.1 %feed.1 = (bf16[1024,1536]{1,0:T(8,128)(2,1)}, bf16[1024,512]{1,0:T(8,128)(2,1)}, bf16[1024,1024]{1,0:T(8,128)(2,1)}) custom-call(bf16[128,1536]{1,0:T(8,128)(2,1)} %copy-done.21, bf16[128,1536]{1,0:T(8,128)(2,1)} %copy-done.33, bf16[128,1536]{1,0:T(8,128)(2,1)} %copy-done.32, bf16[128,1536]{1,0:T(8,128)(2,1)} %copy-done.34, ...), custom_call_target="tpu_custom_call" | custom-call | tf_op jit(solution)/shard_map/feed/pallas_call | solution.py:534
  267.6 5.3 convolution_convert_fusion.6
  291.6 7.2 %outer.1 = bf16[8,4,48,1536]{3,2,1,0:T(8,128)(2,1)} custom-call(s32[8]{0:T(128)} %broadcast_xor_fusion.order_ref, bf16[4,8,48,128]{3,2,1,0:T(8,128)(2,1)} %bitcast.169, bf16[128,1536]{1,0:T(8,128)(2,1)} %copy-done.10), custom_call_target="tpu_custom_call" | custom-call | tf_op jit(solution)/shard_map/outer/pallas_call | solution.py:629
  299.8 7.2 %text_back.1 = (f32[1024,192]{1,0:T(8,128)}, f32[256,192]{1,0:T(8,128)}, f32[256,192]{1,0:T(8,128)}, f32[1,192]{1,0:T(1,128)}) custom-call(s32[8]{0:T(128)} %broadcast_xor_fusion.order_ref, bf16[1024,384]{1,0:T(8,128)(2,1)} %get-tuple-element.113.query_ref.key_ref, f32[1024,192]{1,0:T(8,128)} %get-tuple-element.146.out_ref, ...), custom_call_target="tpu_custom_call" | custom-call | tf_op jit(solution)/shard_map/text_back/pallas_call | solution.py:282
  326.6 10.1 %collective-permute-done.41 = bf16[2,128,768]{2,1,0:T(8,128)(2,1)} collective-permute-done((bf16[2,128,768]{2,1,0:T(8,128)(2,1)S(1)}, bf16[2,128,768]{2,1,0:T(8,128)(2,1)}, u32[]{:S(2)}, u32[]{:S(2)}) %collective-permute-start.41) | collective-permute-done | bytes 393248 | tf_op jit(solution)/shard_map/ppermute | solution.py:650
  336.8 14.0 %attend_back.1 = (f32[1024,192]{1,0:T(8,128)}, f32[1024,192]{1,0:T(8,128)}, f32[1024,192]{1,0:T(8,128)}) custom-call(s32[8]{0:T(128)} %broadcast_xor_fusion.order_ref, bf16[1024,384]{1,0:T(8,128)(2,1)} %get-tuple-element.113.query_ref.key_ref, f32[1024,192]{1,0:T(8,128)} %get-tuple-element.119.own_ref.out_ref, f32[1024,192]{1,0:T(8,128)} %get-tuple-element.157.denom_ref, ...), custom_call_target="tpu_custom_call" | custom-call | tf_op jit(solution)/shard_map/attend_back/pallas_call | solution.py:282
  362.1 10.8 %collective-permute-done.43 = bf16[128,768]{1,0:T(8,128)(2,1)S(1)} collective-permute-done((bf16[128,768]{1,0:T(8,128)(2,1)S(1)}, bf16[128,768]{1,0:T(8,128)(2,1)S(1)}, u32[]{:S(2)}, u32[]{:S(2)}) %collective-permute-start.43) | collective-permute-done | bytes 196640 | tf_op jit(solution)/shard_map/ppermute | solution.py:650
  387.3 7.7 %finish.1 = (bf16[1024,576]{1,0:T(8,128)(2,1)}, f32[1,384]{1,0:T(1,128)}) custom-call(f32[1024,576]{1,0:T(8,128)} %fusion.2.raw_ref, f32[1024,192]{1,0:T(8,128)} %get-tuple-element.166.dquery_ref, f32[1024,192]{1,0:T(8,128)} %get-tuple-element.167.dkey_ref, f32[1024,192]{1,0:T(8,128)} %get-tuple-element.168.dvalue_ref, ...), custom_call_target="tpu_custom_call" | custom-call | tf_op jit(solution)/shard_map/finish/pallas_call | solution.py:339
  410.4 7.8 %head_grads.1 = bf16[1536,960]{1,0:T(8,128)(2,1)} custom-call(bf16[256,1536]{1,0:T(8,128)(2,1)} %bitcast.172, bf16[256,384]{1,0:T(8,128)(2,1)} %get-tuple-element.151.dtext_ref, bf16[1024,1536]{1,0:T(8,128)(2,1)} %get-tuple-element.111.mod_ref, bf16[1024,576]{1,0:T(8,128)(2,1)} %get-tuple-element.173.dqkv_ref), custom_call_target="tpu_custom_call" | custom-call | tf_op jit(solution)/shard_map/head_grads/pallas_call | solution.py:473
  453.7 8.9 %collective-permute-done.65 = bf16[48,1536]{1,0:T(8,128)(2,1)} collective-permute-done((bf16[48,1536]{1,0:T(8,128)(2,1)}, bf16[48,1536]{1,0:T(8,128)(2,1)}, u32[]{:S(2)}, u32[]{:S(2)}) %collective-permute-start.65) | collective-permute-done | bytes 147488 | tf_op jit(solution)/shard_map/ppermute | solution.py:650
  462.6 5.8 %collective-permute-done.66 = bf16[48,1536]{1,0:T(8,128)(2,1)} collective-permute-done((bf16[48,1536]{1,0:T(8,128)(2,1)}, bf16[48,1536]{1,0:T(8,128)(2,1)}, u32[]{:S(2)}, u32[]{:S(2)}) %collective-permute-start.66) | collective-permute-done | bytes 147488 | tf_op jit(solution)/shard_map/ppermute | solution.py:650
  485.8 8.7 %collective-permute-done.55 = f32[12544]{0:T(1024)S(1)} collective-permute-done((f32[12544]{0:T(1024)S(1)}, f32[12544]{0:T(1024)S(1)}, u32[]{:S(2)}, u32[]{:S(2)}) %collective-permute-start.55) | collective-permute-done | bytes 50208 | tf_op jit(solution)/shard_map/ppermute | solution.py:650
  497.9 10.7 %collective-permute-start.60 = (f32[12544]{0:T(1024)S(1)}, f32[12544]{0:T(1024)S(1)}, u32[]{:S(2)}, u32[]{:S(2)}) collective-permute-start(f32[12544]{0:T(1024)S(1)} %add_add_fusion), channel_id=1, source_target_pairs={{0,8},{8,0},{16,24},{24,16},{1,9},{9,1},{17,25},{25,17},{2,10},{10... | collective-permute-start | bytes 150536 | tf_op jit(solution)/shard_map/ppermute | solution.py:650
  (457 shorter events, 307.0 us)
Async XLA Ops:
  7.2 108.0 %all-gather.7.cloned.1.call-start = ((), (), s32[]{:S(2)}) async-start(), calls=%async_computation.16 | async-start | bytes 2703360 | tf_op jit(solution)/shard_map/all_gather | solution.py:809
  16.8 139.0 %all-gather.5.cloned.1.call-start = ((), (), s32[]{:S(2)}) async-start(), calls=%async_computation.15 | async-start | bytes 3932160 | tf_op jit(solution)/shard_map/all_gather | solution.py:809
  29.8 194.7 %all-gather.11.cloned.1.call-start = ((), (), s32[]{:S(2)}) async-start(), calls=%async_computation.18 | async-start | bytes 1966080 | tf_op jit(solution)/shard_map/all_gather | solution.py:809
  51.0 23.2 %collective-permute-start.10 = (bf16[288,1536]{1,0:T(8,128)(2,1)S(1)}, bf16[288,1536]{1,0:T(8,128)(2,1)S(1)}, u32[]{:S(2)}, u32[]{:S(2)}) collective-permute-start(bf16[288,1536]{1,0:T(8,128)(2,1)S(1)} %pad_maximum_fusion.refs_0_), channel_id=1, source_target_pairs={{0,1},{1,0},{2,3},{3,2},{4,5},{5,4},{6,7},{7,6},{8,9},{9,8},{10,11... | collective-permute-start | bytes 2654216 | tf_op jit(solution)/shard_map/ppermute | solution.py:650
  116.3 22.6 %collective-permute-start.20 = (bf16[192,1536]{1,0:T(8,128)(2,1)S(1)}, bf16[192,1536]{1,0:T(8,128)(2,1)}, u32[]{:S(2)}, u32[]{:S(2)}) collective-permute-start(bf16[192,1536]{1,0:T(8,128)(2,1)S(1)} %bitcast.179), channel_id=1, source_target_pairs={{0,4},{1,5},{2,6},{3,7},{4,0},{5,1},{6,2},{7,3},{8,12},{9,13},{10,... | collective-permute-start | bytes 1769480 | tf_op jit(solution)/shard_map/ppermute | solution.py:650
  124.0 25.5 %all-to-all-start.1 = ((bf16[8,32,1536]{2,1,0:T(8,128)(2,1)}), bf16[8,32,1536]{2,1,0:T(8,128)(2,1)S(1)}, u32[]{:S(2)}, u32[]{:S(2)}) async-start(bf16[8,32,1536]{2,1,0:T(8,128)(2,1)} %bitcast.18), calls=%async_computation.1 | async-start | bytes 1572864 | tf_op jit(solution)/shard_map/all_to_all | solution.py:753
  127.6 101.2 %all-gather.9.cloned.1.call-start = ((), (), s32[]{:S(2)}) async-start(), calls=%async_computation.17 | async-start | bytes 3932160 | tf_op jit(solution)/shard_map/all_gather | solution.py:809
  148.9 43.4 %collective-permute-start.23 = (bf16[192,1536]{1,0:T(8,128)(2,1)S(1)}, bf16[192,1536]{1,0:T(8,128)(2,1)}, u32[]{:S(2)}, u32[]{:S(2)}) collective-permute-start(bf16[192,1536]{1,0:T(8,128)(2,1)S(1)} %bitcast.181), channel_id=1, source_target_pairs={{0,2},{1,3},{2,0},{3,1},{4,6},{5,7},{6,4},{7,5},{8,10},{9,11},{10,... | collective-permute-start | bytes 1769480 | tf_op jit(solution)/shard_map/ppermute | solution.py:650
  148.9 43.4 %collective-permute-start.24 = (bf16[192,1536]{1,0:T(8,128)(2,1)}, bf16[192,1536]{1,0:T(8,128)(2,1)}, u32[]{:S(2)}, u32[]{:S(2)}) collective-permute-start(bf16[192,1536]{1,0:T(8,128)(2,1)} %collective-permute-done.19), channel_id=1, source_target_pairs={{0,2},{1,3},{2,0},{3,1},{4,6},{5,7},{6,4},{7,5},{8,10},{9,11},{10,... | collective-permute-start | bytes 1769480 | tf_op jit(solution)/shard_map/ppermute | solution.py:650
  149.4 43.0 %collective-permute-start.25 = (bf16[192,1536]{1,0:T(8,128)(2,1)}, bf16[192,1536]{1,0:T(8,128)(2,1)}, u32[]{:S(2)}, u32[]{:S(2)}) collective-permute-start(bf16[192,1536]{1,0:T(8,128)(2,1)} %collective-permute-done.20), channel_id=1, source_target_pairs={{0,2},{1,3},{2,0},{3,1},{4,6},{5,7},{6,4},{7,5},{8,10},{9,11},{10,... | collective-permute-start | bytes 1769480 | tf_op jit(solution)/shard_map/ppermute | solution.py:650
  150.5 24.9 %all-to-all-start.2 = ((bf16[8,32,1536]{2,1,0:T(8,128)(2,1)}), bf16[8,32,1536]{2,1,0:T(8,128)(2,1)S(1)}, u32[]{:S(2)}, u32[]{:S(2)}) async-start(bf16[8,32,1536]{2,1,0:T(8,128)(2,1)} %broadcast_in_dim.98), calls=%async_computation.2 | async-start | bytes 1572864 | tf_op jit(solution)/shard_map/all_to_all | solution.py:753
  155.3 37.1 %collective-permute-start.26 = (bf16[192,1536]{1,0:T(8,128)(2,1)S(1)}, bf16[192,1536]{1,0:T(8,128)(2,1)}, u32[]{:S(2)}, u32[]{:S(2)}) collective-permute-start(bf16[192,1536]{1,0:T(8,128)(2,1)S(1)} %constant_dynamic-update-slice_fusion.2), channel_id=1, source_target_pairs={{0,2},{1,3},{2,0},{3,1},{4,6},{5,7},{6,4},{7,5},{8,10},{9,11},{10,... | collective-permute-start | bytes 1769480 | tf_op jit(solution)/shard_map/ppermute | solution.py:650
  192.1 188.8 %reduce-scatter.5.cloned.1.call-start = ((), (), s32[]{:S(2)}) async-start(), calls=%async_computation.19 | async-start | bytes 3932160 | tf_op jit(solution)/shard_map/reduce_scatter | solution.py:812
  263.0 169.2 %reduce-scatter.11.cloned.1.call-start = ((), (), s32[]{:S(2)}) async-start(), calls=%async_computation.22 | async-start | bytes 1966080 | tf_op jit(solution)/shard_map/reduce_scatter | solution.py:812
  312.3 38.4 %all-to-all-start.6 = ((bf16[8,32,1536]{2,1,0:T(8,128)(2,1)}), bf16[8,32,1536]{2,1,0:T(8,128)(2,1)}, u32[]{:S(2)}, u32[]{:S(2)}) async-start(bf16[8,32,1536]{2,1,0:T(8,128)(2,1)} %bitcast.201), calls=%async_computation.6 | async-start | bytes 1572864 | tf_op jit(solution)/shard_map/all_to_all | solution.py:753
  321.6 54.3 %collective-permute-start.45 = (bf16[4,192,1536]{2,1,0:T(8,128)(2,1)}, bf16[4,192,1536]{2,1,0:T(8,128)(2,1)}, u32[]{:S(2)}, u32[]{:S(2)}) collective-permute-start(bf16[4,192,1536]{2,1,0:T(8,128)(2,1)} %get-tuple-element.211), channel_id=1, source_target_pairs={{0,2},{1,3},{2,0},{3,1},{4,6},{5,7},{6,4},{7,5},{8,10},{9,11},{10,... | collective-permute-start | bytes 7077896 | tf_op jit(solution)/shard_map/ppermute | solution.py:650
  357.2 113.4 %reduce-scatter.9.cloned.1.call-start = ((), (), s32[]{:S(2)}) async-start(), calls=%async_computation.21 | async-start | bytes 1966080 | tf_op jit(solution)/shard_map/reduce_scatter | solution.py:812
  380.9 22.8 %all-to-all-start.8 = ((bf16[8,48,1024]{2,1,0:T(8,128)(2,1)}), bf16[8,48,1024]{2,1,0:T(8,128)(2,1)}, u32[]{:S(2)}, u32[]{:S(2)}) async-start(bf16[8,48,1024]{2,1,0:T(8,128)(2,1)} %bitcast.200), calls=%async_computation.9 | async-start | bytes 1572864 | tf_op jit(solution)/shard_map/all_to_all | solution.py:753
  385.1 132.5 %reduce-scatter.7.cloned.1.call-start = ((), (), s32[]{:S(2)}) async-start(), calls=%async_computation.20 | async-start | bytes 3932160 | tf_op jit(solution)/shard_map/reduce_scatter | solution.py:812
  403.7 23.0 %collective-permute-start.48 = (bf16[4,128,1536]{2,1,0:T(8,128)(2,1)}, bf16[4,128,1536]{2,1,0:T(8,128)(2,1)}, u32[]{:S(2)}, u32[]{:S(2)}) collective-permute-start(bf16[4,128,1536]{2,1,0:T(8,128)(2,1)} %bitcast.213), channel_id=1, source_target_pairs={{0,2},{1,3},{2,0},{3,1},{4,6},{5,7},{6,4},{7,5},{8,10},{9,11},{10,... | collective-permute-start | bytes 4718600 | tf_op jit(solution)/shard_map/ppermute | solution.py:650
  445.8 22.6 %collective-permute-start.66 = (bf16[48,1536]{1,0:T(8,128)(2,1)}, bf16[48,1536]{1,0:T(8,128)(2,1)}, u32[]{:S(2)}, u32[]{:S(2)}) collective-permute-start(bf16[48,1536]{1,0:T(8,128)(2,1)} %get-tuple-element.235), channel_id=1, source_target_pairs={{0,16},{8,24},{16,0},{24,8},{1,17},{9,25},{17,1},{25,9},{2,18},{10... | collective-permute-start | bytes 442376 | tf_op jit(solution)/shard_map/ppermute | solution.py:650
  452.9 30.0 %collective-permute-start.53 = (f32[12544]{0:T(1024)S(1)}, f32[12544]{0:T(1024)S(1)}, u32[]{:S(2)}, u32[]{:S(2)}) collective-permute-start(f32[12544]{0:T(1024)S(1)} %concatenate.48), channel_id=1, source_target_pairs={{0,1},{1,0},{2,3},{3,2},{4,5},{5,4},{6,7},{7,6},{8,9},{9,8},{10,11... | collective-permute-start | bytes 150536 | tf_op jit(solution)/shard_map/ppermute | solution.py:650
  453.7 30.4 %collective-permute-start.54 = (f32[12544]{0:T(1024)S(1)}, f32[12544]{0:T(1024)S(1)}, u32[]{:S(2)}, u32[]{:S(2)}) collective-permute-start(f32[12544]{0:T(1024)S(1)} %concatenate.48), channel_id=1, source_target_pairs={{0,2},{1,3},{2,0},{3,1},{4,6},{5,7},{6,4},{7,5},{8,10},{9,11},{10,... | collective-permute-start | bytes 150536 | tf_op jit(solution)/shard_map/ppermute | solution.py:650
  475.9 41.7 %all-to-all-start.9 = ((bf16[8,128,512]{2,1,0:T(8,128)(2,1)}), bf16[8,128,512]{2,1,0:T(8,128)(2,1)S(1)}, u32[]{:S(2)}, u32[]{:S(2)}) async-start(bf16[8,128,512]{2,1,0:T(8,128)(2,1)} %bitcast.167), calls=%async_computation.10 | async-start | bytes 2097152 | tf_op jit(solution)/shard_map/all_to_all | solution.py:753
  (134 other events, 1594.6 us)
Sparse Core Ops, SparseCore 0:
  10.2 53.0 all-gather.6
  65.4 62.1 all-gather.4
  129.2 35.7 all-gather.10
  166.4 62.3 all-gather.8
  263.1 57.9 reduce-scatter.4
  323.3 35.3 reduce-scatter.10
  376.1 33.3 reduce-scatter.8
  418.4 68.6 reduce-scatter.6
